TPU v7x, 512 devices: a whole 4x4x16 slice. The times are simulated.
512 devices in a mesh: col: 16 (over y, x), row: 2 (over core), leaf: 16 (over z).
Axes of the slice: x: 4, y: 4, z: 16, core: 2. Of those that a mesh axis runs over, the one named last changes fastest.
Arguments:
- rhs_top: float32 [4, 16, 32, 1024], P(None, 'col', None, 'row'), may hold values from -6 to 6
- diag_inv: bfloat16 [4, 16, 1024, 1024], P(None, 'col', 'row'), may hold values from -1 to 1.25, as said below
- tile_vals: bfloat16 [4, 16, 2, 8, 4, 128, 128], P(None, 'col', None, 'row'), may hold values from -0.1875 to 0.1875
- tile_pattern: int32 [4, 16, 2, 8, 4], P(None, 'col', None, 'row'), may hold values from 0 to 7, as said below
- sub_vals: bfloat16 [16, 16, 2, 8, 4, 128, 128], P('col', 'leaf', None, 'row'), may hold values from -0.1875 to 0.1875
- sub_pattern: int32 [16, 16, 2, 8, 4], P('col', 'leaf', None, 'row'), may hold values from 0 to 7, as said below
- sub_solved: bfloat16 [16, 16, 32, 1024], P('col', 'leaf'), may hold values from -6 to 6
Outputs:
- solved: float32 [4, 16, 32, 1024], P(None, 'col', None, 'row')
- outgoing: float32 [16, 2, 32, 1024], P('col', None, None, 'row')
Inputs may be any that keep to these rules, and one draw needn't show every extreme that they name: `tile_pattern`: in each row block of a panel tile the 4 column blocks are distinct. `sub_pattern`: in each row block of a subtree tile the 4 column blocks are distinct. `diag_inv`: lower triangular.
All inputs are finite; a program needn't handle non-finite values.
Results may differ from a plain program's by a relative error of at most 0.012.
Values may be sent and summed in bfloat16 or wider, within the bound.
No kernel may reach another device: no remote copies, remote signals or barrier semaphores. Data moves between devices by JAX's collectives and lax.ppermute only.
A program may use at most 64 MiB of HBM per device.

v0:
```python
import jax
import jax.numpy as jnp
from jax import lax
from jax.sharding import PartitionSpec as P

STEPS = 4


def padded_to(lines, devices):
    spare = -lines.shape[0] % devices
    if not spare:
        return lines
    return jnp.concatenate([lines, jnp.zeros((spare, *lines.shape[1:]), lines.dtype)])


def laid_out(parts, dim):
    shape = list(parts.shape[1:])
    shape[dim] *= parts.shape[0]
    return jnp.moveaxis(parts, 0, dim).reshape(shape)


def from_everyone(x, axis):
    copies = jnp.broadcast_to(x, (lax.axis_size(axis), *x.shape))
    return lax.all_to_all(copies, axis, split_axis=0, concat_axis=0, tiled=True)


def collect(x, axis, dim):
    return laid_out(from_everyone(x, axis), dim)


def split_up(x, dim, devices):
    before, after = (x.shape[:dim], x.shape[dim + 1 :])
    return jnp.moveaxis(x.reshape(*before, devices, -1, *after), dim, 0)


def sum_at_owner(x, axis, dim):
    parts = split_up(x, dim, lax.axis_size(axis))
    arrived = lax.all_to_all(parts, axis, split_axis=0, concat_axis=0, tiled=True)
    return arrived.sum(axis=0)


def total_of(x, axes):
    lines = x.reshape(-1, x.shape[-1])
    padded = padded_to(lines, lax.axis_size(axes))
    whole = collect(sum_at_owner(padded, axes, 0), axes, 0)
    return lax.slice_in_dim(whole, 0, len(lines)).reshape(x.shape)


def from_behind(block, axis, distance):
    devices = range(lax.axis_size(axis))
    route = [((i - distance) % len(devices), i) for i in devices]
    return lax.ppermute(block, axis, route)


def apply_tiles(vectors, values, pattern):
    nrows, width = vectors.shape
    block = values.shape[-1]
    blocks = vectors.reshape(nrows, width // block, block).transpose(1, 0, 2)
    chosen = blocks[pattern]
    result = jnp.einsum("hbkri,hbkij->hrbj", chosen, values, preferred_element_type=jnp.float32)
    return result.reshape(2, nrows, values.shape[1] * block)


def panel_update(rhs_b, inverse, values, pattern):
    whole = lax.all_gather(rhs_b, "row", axis=1, tiled=True)
    full_solved = lax.dot_general(
        whole, inverse, (((1,), (1,)), ((), ())), preferred_element_type=jnp.float32
    )
    width = rhs_b.shape[1]
    solved = lax.dynamic_slice_in_dim(full_solved, lax.axis_index("row") * width, width, 1)
    return (solved, apply_tiles(full_solved.astype(jnp.bfloat16), values, pattern))


def per_device(rhs_top, diag_inv, tile_vals, tile_pattern, sub_vals, sub_pattern, sub_solved):
    inverses = lax.all_gather(diag_inv, "row", axis=2, tiled=True)
    partial_value = apply_tiles(sub_solved[0, 0], sub_vals[0, 0], sub_pattern[0, 0])
    merged = total_of(partial_value, "leaf")
    outputs = []
    recv_first = merged[0]
    recv_second = merged[1]
    for level in range(STEPS):
        rhs_b = (rhs_top[level, 0] - recv_first).astype(jnp.bfloat16)
        solved, update = panel_update(
            rhs_b, inverses[level, 0], tile_vals[level, 0], tile_pattern[level, 0]
        )
        outputs.append(solved)
        sending = jnp.stack([update[0] + recv_second, update[1]], axis=0)
        moved = from_behind(sending, "col", 1)
        recv_first = moved[0]
        recv_second = moved[1]
    final_pair = jnp.stack([recv_first, recv_second], axis=0)
    solved_all = jnp.stack(outputs, axis=0)[:, None]
    return (solved_all, final_pair[None])


def solution(mesh):
    placed = (
        P(None, "col", None, "row"),
        P(None, "col", "row", None),
        P(None, "col", None, "row", None, None, None),
        P(None, "col", None, "row", None),
        P("col", "leaf", None, "row", None, None, None),
        P("col", "leaf", None, "row", None),
        P("col", "leaf", None, None),
    )
    return jax.shard_map(
        per_device,
        mesh=mesh,
        in_specs=placed,
        out_specs=(P(None, "col", None, "row"), P("col", None, None, "row")),
        check_vma=False,
    )
```

profile of v0, /device:TPU:1, one launch (start us, length us, event | category | flops | bytes accessed | tf_op | source)
XLA Modules:
  0.0 135.8 jit_solution(13684946997240699190)
XLA Ops:
  7.3 0.7 all-gather.2.cloned.1.call-update
  8.2 0.6 gather_fusion
  9.3 27.5 %all_to_all.10 = f32[16,4,512]{2,1,0:T(4,128)S(1)} all-to-all(f32[16,4,512]{2,1,0:T(4,128)S(1)} %reshape_reshape_reshape.3), channel_id=1, replica_groups=mesh['col'=16,'row'=2,'leaf'=16] {'leaf'}, dimensions={0} | all-to-all | bytes 262144 | tf_op jit(solution)/shard_map/all_to_all | solution.py:38
  36.8 0.7 broadcast_in_dim.6
  37.5 6.0 %all-to-all-start.1 = ((f32[16,4,512]{2,1,0:T(4,128)}), f32[16,4,512]{2,1,0:T(4,128)S(1)}, u32[]{:S(2)}, u32[]{:S(2)}) async-start(f32[16,4,512]{2,1,0:T(4,128)} %broadcast_in_dim.6), calls=%async_computation.1 | async-start | bytes 262144 | tf_op jit(solution)/shard_map/all_to_all | solution.py:24
  43.7 11.8 %all-to-all-done.1 = f32[16,4,512]{2,1,0:T(4,128)S(1)} async-done(((f32[16,4,512]{2,1,0:T(4,128)}), f32[16,4,512]{2,1,0:T(4,128)S(1)}, u32[]{:S(2)}, u32[]{:S(2)}) %all-to-all-start.1) | async-done | bytes 131104 | tf_op jit(solution)/shard_map/all_to_all | solution.py:24
  55.6 5.3 %all_gather.15 = bf16[32,1024]{1,0:T(8,128)(2,1)S(1)} all-gather(bf16[32,512]{1,0:T(8,128)(2,1)S(1)} %fusion.16), channel_id=1, replica_groups=mesh['col'=16,'row'=2,'leaf'=16] {'row'}, dimensions={1}, use_global_device_ids=true | all-gather | bytes 98304 | tf_op jit(solution)/shard_map/all_gather | solution.py:65
  60.9 2.3 %fusion.3 = f32[32,1024]{1,0:T(8,128)S(1)} fusion(bf16[32,1024]{1,0:T(8,128)(2,1)S(1)} %all_gather.15, bf16[4,1,1024,1024]{3,2,1,0:T(8,128)(2,1)} %all-gather.2.cloned.1.call-done), kind=kOutput, calls=%fused_computation.12 | convolution fusion | flops 67108864 | bytes 2293760 | tf_op jit(solution)/shard_map/dot_general | solution.py:66
  63.3 0.6 gather_fusion.1
  63.9 1.5 %convolution_bitcast_fusion.3 = f32[2,32,4,128]{3,1,2,0:T(8,128)S(1)} fusion(bf16[2,4,4,32,128]{4,3,2,1,0:T(8,128)(2,1)S(1)} %bitcast.164, bf16[4,1,2,4,4,128,128]{6,5,4,3,2,1,0:T(8,128)(2,1)} %param.9), kind=kOutput, calls=%fused_computation.16 | convolution fusion | flops 33554432 | bytes 1441792 | tf_op jit(solution)/shard_map/hbkri,hbkij->hrbj/dot_general | solution.py:60
  65.7 3.1 %collective-permute-start = (f32[2,32,512]{2,0,1:T(2,128)S(1)}, f32[2,32,512]{2,0,1:T(2,128)S(1)}, u32[]{:S(2)}, u32[]{:S(2)}) collective-permute-start(f32[2,32,512]{2,0,1:T(2,128)S(1)} %pad_maximum_fusion), channel_id=1, source_target_pairs={{480,0},{0,32},{32,64},{64,96},{96,128},{128,160},{160,192},{192,2... | collective-permute-start | bytes 393224 | tf_op jit(solution)/shard_map/ppermute | solution.py:52
  69.0 6.9 %collective-permute-done = f32[2,32,512]{2,0,1:T(2,128)S(1)} collective-permute-done((f32[2,32,512]{2,0,1:T(2,128)S(1)}, f32[2,32,512]{2,0,1:T(2,128)S(1)}, u32[]{:S(2)}, u32[]{:S(2)}) %collective-permute-start) | collective-permute-done | bytes 131104 | tf_op jit(solution)/shard_map/ppermute | solution.py:52
  76.0 2.6 %all_gather.17 = bf16[32,1024]{1,0:T(8,128)(2,1)S(1)} all-gather(bf16[32,512]{1,0:T(8,128)(2,1)S(1)} %fusion.15), channel_id=1, replica_groups=mesh['col'=16,'row'=2,'leaf'=16] {'row'}, dimensions={1}, use_global_device_ids=true | all-gather | bytes 98304 | tf_op jit(solution)/shard_map/all_gather | solution.py:65
  78.5 2.3 %fusion.2 = f32[32,1024]{1,0:T(8,128)S(1)} fusion(bf16[32,1024]{1,0:T(8,128)(2,1)S(1)} %all_gather.17, bf16[4,1,1024,1024]{3,2,1,0:T(8,128)(2,1)} %all-gather.2.cloned.1.call-done), kind=kOutput, calls=%fused_computation.10 | convolution fusion | flops 67108864 | bytes 2293760 | tf_op jit(solution)/shard_map/dot_general | solution.py:66
  80.9 0.6 gather_fusion.2
  81.5 1.5 %convolution_bitcast_fusion.2 = f32[2,32,4,128]{3,1,2,0:T(8,128)S(1)} fusion(bf16[2,4,4,32,128]{4,3,2,1,0:T(8,128)(2,1)S(1)} %bitcast.165, bf16[4,1,2,4,4,128,128]{6,5,4,3,2,1,0:T(8,128)(2,1)} %param.9), kind=kOutput, calls=%fused_computation.15 | convolution fusion | flops 33554432 | bytes 1441792 | tf_op jit(solution)/shard_map/hbkri,hbkij->hrbj/dot_general | solution.py:60
  83.4 1.9 %collective-permute-start.1 = (f32[2,32,512]{2,0,1:T(2,128)S(1)}, f32[2,32,512]{2,0,1:T(2,128)S(1)}, u32[]{:S(2)}, u32[]{:S(2)}) collective-permute-start(f32[2,32,512]{2,0,1:T(2,128)S(1)} %pad_maximum_fusion.1), channel_id=1, source_target_pairs={{480,0},{0,32},{32,64},{64,96},{96,128},{128,160},{160,192},{192,2... | collective-permute-start | bytes 393224 | tf_op jit(solution)/shard_map/ppermute | solution.py:52
  85.3 7.9 %collective-permute-done.1 = f32[2,32,512]{2,0,1:T(2,128)S(1)} collective-permute-done((f32[2,32,512]{2,0,1:T(2,128)S(1)}, f32[2,32,512]{2,0,1:T(2,128)S(1)}, u32[]{:S(2)}, u32[]{:S(2)}) %collective-permute-start.1) | collective-permute-done | bytes 131104 | tf_op jit(solution)/shard_map/ppermute | solution.py:52
  93.3 2.7 %all_gather.18 = bf16[32,1024]{1,0:T(8,128)(2,1)S(1)} all-gather(bf16[32,512]{1,0:T(8,128)(2,1)S(1)} %fusion.14), channel_id=1, replica_groups=mesh['col'=16,'row'=2,'leaf'=16] {'row'}, dimensions={1}, use_global_device_ids=true | all-gather | bytes 98304 | tf_op jit(solution)/shard_map/all_gather | solution.py:65
  96.1 2.3 %fusion.1 = f32[32,1024]{1,0:T(8,128)S(1)} fusion(bf16[32,1024]{1,0:T(8,128)(2,1)S(1)} %all_gather.18, bf16[4,1,1024,1024]{3,2,1,0:T(8,128)(2,1)} %all-gather.2.cloned.1.call-done), kind=kOutput, calls=%fused_computation.8 | convolution fusion | flops 67108864 | bytes 2293760 | tf_op jit(solution)/shard_map/dot_general | solution.py:66
  98.4 0.6 gather_fusion.3
  99.0 1.5 %convolution_bitcast_fusion.1 = f32[2,32,4,128]{3,1,2,0:T(8,128)S(1)} fusion(bf16[2,4,4,32,128]{4,3,2,1,0:T(8,128)(2,1)S(1)} %bitcast.166, bf16[4,1,2,4,4,128,128]{6,5,4,3,2,1,0:T(8,128)(2,1)} %param.9), kind=kOutput, calls=%fused_computation.14 | convolution fusion | flops 33554432 | bytes 1441792 | tf_op jit(solution)/shard_map/hbkri,hbkij->hrbj/dot_general | solution.py:60
  100.9 1.9 %collective-permute-start.2 = (f32[2,32,512]{2,0,1:T(2,128)S(1)}, f32[2,32,512]{2,0,1:T(2,128)S(1)}, u32[]{:S(2)}, u32[]{:S(2)}) collective-permute-start(f32[2,32,512]{2,0,1:T(2,128)S(1)} %pad_maximum_fusion.2), channel_id=1, source_target_pairs={{480,0},{0,32},{32,64},{64,96},{96,128},{128,160},{160,192},{192,2... | collective-permute-start | bytes 393224 | tf_op jit(solution)/shard_map/ppermute | solution.py:52
  102.9 7.9 %collective-permute-done.2 = f32[2,32,512]{2,0,1:T(2,128)S(1)} collective-permute-done((f32[2,32,512]{2,0,1:T(2,128)S(1)}, f32[2,32,512]{2,0,1:T(2,128)S(1)}, u32[]{:S(2)}, u32[]{:S(2)}) %collective-permute-start.2) | collective-permute-done | bytes 131104 | tf_op jit(solution)/shard_map/ppermute | solution.py:52
  110.9 2.7 %all_gather.19 = bf16[32,1024]{1,0:T(8,128)(2,1)S(1)} all-gather(bf16[32,512]{1,0:T(8,128)(2,1)S(1)} %fusion.13), channel_id=1, replica_groups=mesh['col'=16,'row'=2,'leaf'=16] {'row'}, dimensions={1}, use_global_device_ids=true | all-gather | bytes 98304 | tf_op jit(solution)/shard_map/all_gather | solution.py:65
  113.6 2.3 %fusion = f32[32,1024]{1,0:T(8,128)S(1)} fusion(bf16[32,1024]{1,0:T(8,128)(2,1)S(1)} %all_gather.19, bf16[4,1,1024,1024]{3,2,1,0:T(8,128)(2,1)} %all-gather.2.cloned.1.call-done), kind=kOutput, calls=%fused_computation.6 | convolution fusion | flops 67108864 | bytes 2293760 | tf_op jit(solution)/shard_map/dot_general | solution.py:66
  115.9 0.6 gather_fusion.4
  116.5 1.5 %convolution_bitcast_fusion = f32[2,32,4,128]{3,1,2,0:T(8,128)S(1)} fusion(bf16[2,4,4,32,128]{4,3,2,1,0:T(8,128)(2,1)S(1)} %bitcast.167, bf16[4,1,2,4,4,128,128]{6,5,4,3,2,1,0:T(8,128)(2,1)} %param.9), kind=kOutput, calls=%fused_computation.13 | convolution fusion | flops 33554432 | bytes 1441792 | tf_op jit(solution)/shard_map/hbkri,hbkij->hrbj/dot_general | solution.py:60
  118.4 1.9 %collective-permute-start.3 = (f32[2,32,512]{2,0,1:T(2,128)S(1)}, f32[2,32,512]{2,0,1:T(2,128)S(1)}, u32[]{:S(2)}, u32[]{:S(2)}) collective-permute-start(f32[2,32,512]{2,0,1:T(2,128)S(1)} %pad_maximum_fusion.3), channel_id=1, source_target_pairs={{480,0},{0,32},{32,64},{64,96},{96,128},{128,160},{160,192},{192,2... | collective-permute-start | bytes 393224 | tf_op jit(solution)/shard_map/ppermute | solution.py:52
  120.3 0.7 maximum_bitcast_fusion
  121.1 7.2 %collective-permute-done.3 = f32[2,32,512]{2,0,1:T(2,128)S(1)} collective-permute-done((f32[2,32,512]{2,0,1:T(2,128)S(1)}, f32[2,32,512]{2,0,1:T(2,128)S(1)}, u32[]{:S(2)}, u32[]{:S(2)}) %collective-permute-start.3) | collective-permute-done | bytes 131104 | tf_op jit(solution)/shard_map/ppermute | solution.py:52
  128.3 0.7 copy.42
  (68 shorter events, 2.8 us)
Async XLA Ops:
  7.2 1.6 %copy-start = (bf16[1,1,2,4,4,128,128]{6,5,4,3,2,1,0:T(8,128)(2,1)S(1)}, bf16[1,1,2,4,4,128,128]{6,5,4,3,2,1,0:T(8,128)(2,1)}, u32[]{:S(2)}) copy-start(bf16[1,1,2,4,4,128,128]{6,5,4,3,2,1,0:T(8,128)(2,1)} %param.11) | copy-start | bytes 3145732
  7.2 0.8 copy-start.4
  7.2 0.9 copy-start.2
  7.2 36.3 %copy-start.3 = (s32[4,1,2,4,4]{4,3,2,1,0:T(4,128)S(1)}, s32[4,1,2,4,4]{4,3,2,1,0:T(4,128)}, u32[]{:S(2)}) copy-start(s32[4,1,2,4,4]{4,3,2,1,0:T(4,128)} %param.10) | copy-start | bytes 1540
  7.2 48.4 %copy-start.1 = (f32[4,1,32,512]{3,2,1,0:T(8,128)S(1)}, f32[4,1,32,512]{3,2,1,0:T(8,128)}, u32[]{:S(2)}) copy-start(f32[4,1,32,512]{3,2,1,0:T(8,128)} %param.7) | copy-start | bytes 786436
  7.2 53.7 %all-gather.2.cloned.1.call-start = ((), (), s32[]{:S(2)}) async-start(), calls=%async_computation.2 | async-start | bytes 12582912 | tf_op jit(solution)/shard_map/all_gather | solution.py:75
  37.5 18.0 %all-to-all-start.1 = ((f32[16,4,512]{2,1,0:T(4,128)}), f32[16,4,512]{2,1,0:T(4,128)S(1)}, u32[]{:S(2)}, u32[]{:S(2)}) async-start(f32[16,4,512]{2,1,0:T(4,128)} %broadcast_in_dim.6), calls=%async_computation.1 | async-start | bytes 262144 | tf_op jit(solution)/shard_map/all_to_all | solution.py:24
  65.7 10.2 %collective-permute-start = (f32[2,32,512]{2,0,1:T(2,128)S(1)}, f32[2,32,512]{2,0,1:T(2,128)S(1)}, u32[]{:S(2)}, u32[]{:S(2)}) collective-permute-start(f32[2,32,512]{2,0,1:T(2,128)S(1)} %pad_maximum_fusion), channel_id=1, source_target_pairs={{480,0},{0,32},{32,64},{64,96},{96,128},{128,160},{160,192},{192,2... | collective-permute-start | bytes 393224 | tf_op jit(solution)/shard_map/ppermute | solution.py:52
  83.4 9.9 %collective-permute-start.1 = (f32[2,32,512]{2,0,1:T(2,128)S(1)}, f32[2,32,512]{2,0,1:T(2,128)S(1)}, u32[]{:S(2)}, u32[]{:S(2)}) collective-permute-start(f32[2,32,512]{2,0,1:T(2,128)S(1)} %pad_maximum_fusion.1), channel_id=1, source_target_pairs={{480,0},{0,32},{32,64},{64,96},{96,128},{128,160},{160,192},{192,2... | collective-permute-start | bytes 393224 | tf_op jit(solution)/shard_map/ppermute | solution.py:52
  100.9 9.9 %collective-permute-start.2 = (f32[2,32,512]{2,0,1:T(2,128)S(1)}, f32[2,32,512]{2,0,1:T(2,128)S(1)}, u32[]{:S(2)}, u32[]{:S(2)}) collective-permute-start(f32[2,32,512]{2,0,1:T(2,128)S(1)} %pad_maximum_fusion.2), channel_id=1, source_target_pairs={{480,0},{0,32},{32,64},{64,96},{96,128},{128,160},{160,192},{192,2... | collective-permute-start | bytes 393224 | tf_op jit(solution)/shard_map/ppermute | solution.py:52
  118.4 9.9 %collective-permute-start.3 = (f32[2,32,512]{2,0,1:T(2,128)S(1)}, f32[2,32,512]{2,0,1:T(2,128)S(1)}, u32[]{:S(2)}, u32[]{:S(2)}) collective-permute-start(f32[2,32,512]{2,0,1:T(2,128)S(1)} %pad_maximum_fusion.3), channel_id=1, source_target_pairs={{480,0},{0,32},{32,64},{64,96},{96,128},{128,160},{160,192},{192,2... | collective-permute-start | bytes 393224 | tf_op jit(solution)/shard_map/ppermute | solution.py:52
Sparse Core Ops, SparseCore 0:
  10.1 37.0 all-gather.1
where the time goes:
time: 136 us
  waiting for transfers between devices  42.5 us (31%)
  blocking collectives  40.8 us (30%)
  matrix products  15.5 us (11%)
  starting transfers between devices  14.9 us (11%)
  between operations  14.6 us (11%)
  local copies, waits for them, and re-layouts  5.79 us (4%)
  other arithmetic  1.83 us (1%)
    ppermute x4, waiting for transfers between devices, from_behind(): return lax.ppermute(block, axis, route)  30 us
    all_to_all x1, blocking collectives, sum_at_owner(): lax.all_to_all(parts, axis, split_axis=0, concat_axis=0, tiled=True)  27.5 us
    all_gather x4, blocking collectives, panel_update(): whole = lax.all_gather(rhs_b, 'row', axis=1, tiled=True)  13.3 us
    all_to_all x1, waiting for transfers between devices, from_everyone(): return lax.all_to_all(copies, axis, split_axis=0, concat_axis=0, tiled=True)  11.8 us
    dot_general x4, matrix products, panel_update(): lax.dot_general(whole, inverse, (((1,), (1,)), ((), ())), preferred_eleme...  9.21 us
    ppermute x4, starting transfers between devices, from_behind(): return lax.ppermute(block, axis, route)  8.88 us
    dot_general x5, matrix products, apply_tiles(): jnp.einsum('hbkri,hbkij->hrbj', chosen, values, preferred_element_type=jn...  6.27 us
    all_to_all x1, starting transfers between devices, from_everyone(): return lax.all_to_all(copies, axis, split_axis=0, concat_axis=0, tiled=True)  6.01 us
  transfers between devices with their start and end apart: 6, of which 5 were waited for; matrix products, arithmetic and copies ran while one was open for 2% of the time, Pallas kernels for 0%

commit v1 on v0

v1 whole, which is shorter than its diff:
```python
import functools

import jax
import jax.numpy as jnp
from jax import lax
from jax.experimental import pallas as pl
from jax.experimental.pallas import tpu as pltpu
from jax.sharding import PartitionSpec as P


STEPS = 4
BLK = 128
NB = 4
HALF = NB * BLK
NRHS = 32
NEAR = 4
RING = 4
LIMIT = 44
EDGE = 48
F32 = jnp.float32
BF16 = jnp.bfloat16

vmem = pl.BlockSpec(memory_space=pltpu.VMEM)
smem = pl.BlockSpec(memory_space=pltpu.SMEM)
hbm = pl.BlockSpec(memory_space=pltpu.HBM)


def dot(lhs, rhs, side):
    return lax.dot_general(lhs, rhs, (((1,), (side,)), ((), ())), preferred_element_type=F32)


def subtree_kernel(pat, solved, vals, out):
    for h in range(2):
        for b in range(NB):
            cols = [pl.multiple_of(pat[0, 0, h, b, k] * BLK, BLK) for k in range(NB)]
            lhs = jnp.concatenate([solved[:, pl.ds(c, BLK)] for c in cols], axis=1)
            part = dot(lhs, vals[h, b], 0).astype(BF16)
            for copy in range(out.shape[0]):
                out[copy, h, :, b * BLK : (b + 1) * BLK] = part


def merge_kernel(parts, out):
    total = parts[0].astype(F32)
    for i in range(1, parts.shape[0]):
        total = total + parts[i].astype(F32)
    total = total.astype(out.dtype)
    for copy in range(out.shape[0]):
        out[copy] = total


def panel_copies(level, own, other, tiles, inverse, held, sems):
    me = lax.axis_index("row")
    waits = []
    for part in range(4):
        lo, width = (part % 2) * 256, (part + 1) * 256
        dst = inverse.at[part * 256 : (part + 1) * 256, :width]
        mine, theirs = (
            pltpu.make_async_copy(src.at[level, lo : lo + 256, :width], dst, sems.at[part])
            for src in (own, other)
        )
        pl.when(me == part // 2)(mine.start)
        pl.when(me != part // 2)(theirs.start)
        waits.append(mine.wait)
    last = pltpu.make_async_copy(tiles.at[level], held, sems.at[4])
    last.start()
    return waits + [last.wait]


def level_kernel(level, front, whole, carry, pat, own, other, tiles, *refs):
    refs = list(refs)
    passed = None if front else (refs.pop(0), refs.pop(0))
    here = None if level == 0 else (refs.pop(0), refs.pop(0))
    solved, send = refs.pop(0), refs.pop(0)
    ahead = (refs.pop(0), refs.pop(0)) if level < STEPS - 1 else None
    blocks, picks, sems, ahead_sems = refs[:4]
    behind = lax.rem(lax.axis_index("col"), RING) == 0

    def work():
        inverse, held = here or (refs[4], refs[5])
        pattern = pltpu.make_async_copy(pat, picks, sems.at[5])
        pattern.start()
        waits = [lambda: None] * 5
        if here is None:
            waits = panel_copies(level, own, other, tiles, inverse, held, sems)
        later = panel_copies(level + 1, own, other, tiles, *ahead, ahead_sems) if ahead else []
        me = lax.axis_index("row")
        rhs = jnp.concatenate([whole[0], whole[1]], axis=1)
        for part in range(4):
            waits[part]()
            lo, width = part * 256, (part + 1) * 256
            x = dot(rhs[:, :width], inverse[lo : lo + 256, :width], 1)
            for q in range(2):
                blocks[part * 2 + q] = x[:, q * BLK : (q + 1) * BLK].astype(BF16)

            @pl.when(me == part // 2)
            def _():
                solved[:, (part % 2) * 256 : (part % 2) * 256 + 256] = x

        pattern.wait()
        waits[4]()
        for h in range(2):
            for b in range(NB):
                base = ((level * 2 + h) * NB + b) * NB
                lhs = jnp.concatenate([blocks[picks[base + k]] for k in range(NB)], axis=1)
                out = dot(lhs, held[h, b], 0)
                at = (slice(None), slice(b * BLK, (b + 1) * BLK))
                if h == 0:
                    out = out + carry[(1, *at)].astype(F32)
                send[(h, *at)] = out.astype(BF16)
        for wait in later:
            wait()

    if front:
        pl.when(jnp.logical_not(behind))(work)
    else:
        pl.when(behind)(work)

        @pl.when(jnp.logical_not(behind))
        def _():
            solved[...] = passed[0][...]
            send[...] = passed[1][...]


def call(kernel, out, in_specs, scratch=(), flops=0, moved=0, limit=None):
    many = isinstance(out, (tuple, list))
    return pl.pallas_call(
        kernel,
        out_shape=out,
        in_specs=in_specs,
        out_specs=[vmem] * len(out) if many else vmem,
        scratch_shapes=list(scratch),
        compiler_params=pltpu.CompilerParams(vmem_limit_bytes=limit),
        cost_estimate=pl.CostEstimate(flops=flops, bytes_accessed=moved, transcendentals=0),
    )


def exchange(parts, groups):
    return lax.all_to_all(
        parts, "leaf", split_axis=0, concat_axis=0, tiled=True, axis_index_groups=groups
    )


def chain(rhs_top, diag_inv, tile_vals, tile_pattern, sub_vals, sub_pattern, sub_solved):
    leaves = lax.axis_size("leaf")
    cols = lax.axis_size("col")
    state = (2, NRHS, HALF)
    near = [list(range(i, i + NEAR)) for i in range(0, leaves, NEAR)]
    far = [list(range(i, leaves, NEAR)) for i in range(NEAR)]
    copies = call(
        subtree_kernel,
        jax.ShapeDtypeStruct((len(near[0]), *state), BF16),
        [smem, vmem, vmem],
        flops=2 * 32 * 32 * 128 * 128,
        moved=1 << 20,
    )(sub_pattern, sub_solved[0, 0], sub_vals.reshape(2, NB, NB * BLK, BLK))
    arrived = exchange(copies, near)
    copies = call(
        merge_kernel,
        jax.ShapeDtypeStruct((len(far[0]), *state), BF16),
        [vmem],
        moved=1 << 19,
        limit=8 << 20,
    )(arrived)
    arrived = exchange(copies, far)
    carry = call(
        merge_kernel,
        jax.ShapeDtypeStruct((1, *state), F32),
        [vmem],
        moved=1 << 19,
        limit=8 << 20,
    )(arrived)[0]
    own = diag_inv[:, 0]
    other = lax.ppermute(own, "row", [(0, 1), (1, 0)])
    tiles = tile_vals[:, 0].reshape(STEPS, 2, NB, NB * BLK, BLK)
    panel = (
        jax.ShapeDtypeStruct((2 * HALF, 2 * HALF), BF16),
        jax.ShapeDtypeStruct((2, NB, NB * BLK, BLK), BF16),
    )
    pattern = tile_pattern.reshape(-1)
    across = [(c, (c + 1) % cols) for c in range(RING - 1, cols, RING)]
    along = [(c, c + 1) for c in range(cols) if c % RING != RING - 1]
    solves, weights = [], {True: [], False: []}
    carries = {True: carry, False: carry}
    for level in range(STEPS):
        total = carry[0] if level == 0 else carries[True][0] + carries[False][0]
        rhs = (rhs_top[level, 0] - total.astype(F32)).astype(BF16)
        whole = lax.all_gather(rhs, "row", axis=0, tiled=False)
        last = level == STEPS - 1
        passed = []
        arrived = {}
        for front in (True, False):
            solved, send, *weights[front] = call(
                functools.partial(level_kernel, level, front),
                (
                    jax.ShapeDtypeStruct((NRHS, HALF), F32),
                    jax.ShapeDtypeStruct(state, BF16),
                    *(() if last else panel),
                ),
                [vmem, vmem, hbm, hbm, hbm, hbm] + [vmem] * len(passed + weights[front]),
                [
                    pltpu.VMEM((2 * NB, NRHS, BLK), BF16),
                    pltpu.SMEM(pattern.shape, jnp.int32),
                    pltpu.SemaphoreType.DMA((6,)),
                    pltpu.SemaphoreType.DMA((5,)),
                    *(pltpu.VMEM(p.shape, p.dtype) for p in panel if level == 0),
                ],
                flops=2 * 32 * (1 << 20),
                moved=3 << 20,
                limit=(EDGE if level in (0, STEPS - 1) else LIMIT) << 20,
            )(
                whole,
                carries[front],
                pattern,
                own,
                other,
                tiles,
                *passed,
                *weights[front],
            )
            passed = [solved, send]
            arrived[not front] = lax.ppermute(send, "col", across if front else along)
        solves.append(solved)
        carries = arrived
    outgoing = carries[True].astype(F32) + carries[False].astype(F32)
    return jnp.stack(solves, axis=0)[:, None], outgoing[None]


def solution(mesh):
    placed = (
        P(None, "col", None, "row"),
        P(None, "col", "row", None),
        P(None, "col", None, "row", None, None, None),
        P(None, "col", None, "row", None),
        P("col", "leaf", None, "row", None, None, None),
        P("col", "leaf", None, "row", None),
        P("col", "leaf", None, None),
    )
    return jax.shard_map(
        chain,
        mesh=mesh,
        in_specs=placed,
        out_specs=(P(None, "col", None, "row"), P("col", None, None, "row")),
        check_vma=False,
    )
```

time: 136 us -> 108 us (0.79)
  matrix products: 15.5 us -> 0 us
  starting transfers between devices: 14.9 us -> 29.9 us
  blocking collectives: 40.8 us -> 26.2 us
  between operations: 14.6 us -> 0.82 us
  Pallas kernels: 0 us -> 11.2 us
  local copies, waits for them, and re-layouts: 5.79 us -> 0.11 us
  waiting for transfers between devices: 42.5 us -> 37.2 us
    dot_general x9 -> x0, matrix products: 15.5 us -> none  [the longest x4 9.21 us: panel_update(): lax.dot_general(whole, inverse, (((1,), (1,)), ((), ())), preferred_eleme...]
    all_to_all x1, blocking collectives: 27.5 us -> 12 us  [exchange(): lax.all_to_all(parts, 'leaf', split_axis=0, concat_axis=0, tiled=True, ax...]
    ppermute x4 -> x9, starting transfers between devices: 8.88 us -> 20.4 us  [the longest x8 11.5 us: chain(): arrived[not front] = lax.ppermute(send, 'col', across if front else along)]
    pallas_call x0 -> x11, Pallas kernels: none -> 11.2 us  [the longest x8 8.14 us: chain(): call(functools.partial(level_kernel, level, front), (jax.ShapeDtypeStruct...]
    ppermute x4 -> x9, waiting for transfers between devices: 30 us -> 21.8 us  [the longest x8 21.8 us: chain(): arrived[not front] = lax.ppermute(send, 'col', across if front else along)]
    all_to_all x1, waiting for transfers between devices: 11.8 us -> 15.4 us  [exchange(): lax.all_to_all(parts, 'leaf', split_axis=0, concat_axis=0, tiled=True, ax...]
    all_to_all x1, starting transfers between devices: 6.01 us -> 9.46 us  [exchange(): lax.all_to_all(parts, 'leaf', split_axis=0, concat_axis=0, tiled=True, ax...]
    gather x5 -> x0, local copies, waits for them, and re-layouts: 3.01 us -> none  [apply_tiles(): chosen = blocks[pattern]]
  transfers between devices with their start and end apart: 6 -> 10, of which waited for: 5 -> 6; matrix products, arithmetic and copies ran while one was open for 2% -> 1% of each run, Pallas kernels for 0% -> 7%
where the time goes in v1:
time: 108 us; the launch traced here: 107 us
  waiting for transfers between devices  37.2 us (34%)
  starting transfers between devices  29.9 us (28%)
  blocking collectives  26.2 us (24%)
  Pallas kernels  11.2 us (10%)
  other arithmetic  1.45 us (1%)
    ppermute x8, waiting for transfers between devices, chain(): arrived[not front] = lax.ppermute(send, 'col', across if front else along)  21.8 us
    all_to_all x1, waiting for transfers between devices, exchange(): lax.all_to_all(parts, 'leaf', split_axis=0, concat_axis=0, tiled=True, ax...  15.4 us
    all_gather x4, blocking collectives, chain(): whole = lax.all_gather(rhs, 'row', axis=0, tiled=False)  14.2 us
    all_to_all x1, blocking collectives, exchange(): lax.all_to_all(parts, 'leaf', split_axis=0, concat_axis=0, tiled=True, ax...  12 us
    ppermute x8, starting transfers between devices, chain(): arrived[not front] = lax.ppermute(send, 'col', across if front else along)  11.5 us
    all_to_all x1, starting transfers between devices, exchange(): lax.all_to_all(parts, 'leaf', split_axis=0, concat_axis=0, tiled=True, ax...  9.46 us
    ppermute x1, starting transfers between devices, chain(): other = lax.ppermute(own, 'row', [(0, 1), (1, 0)])  8.88 us
    pallas_call x8, Pallas kernels, chain(): call(functools.partial(level_kernel, level, front), (jax.ShapeDtypeStruct...  8.14 us
  transfers between devices with their start and end apart: 10, of which 6 were waited for; matrix products, arithmetic and copies ran while one was open for 1% of the time, Pallas kernels for 7%

profile of v1, /device:TPU:1, one launch (start us, length us, event | category | flops | bytes accessed | tf_op | source)
XLA Modules:
  0.0 106.8 jit_solution(12234166258865519006)
XLA Ops:
  0.7 8.9 %collective-permute-start = (bf16[4,512,1024]{2,1,0:T(8,128)(2,1)}, bf16[4,512,1024]{2,1,0:T(8,128)(2,1)}, u32[]{:S(2)}, u32[]{:S(2)}) collective-permute-start(bf16[4,512,1024]{2,1,0:T(8,128)(2,1)} %bitcast.36), channel_id=1, source_target_pairs={{0,16},{16,0},{1,17},{17,1},{2,18},{18,2},{3,19},{19,3},{4,20},{20... | collective-permute-start | bytes 12582920 | tf_op jit(solution)/shard_map/ppermute | solution.py:173
  9.5 2.3 %shard_map.86 = bf16[4,2,32,512]{3,2,1,0:T(8,128)(2,1)} custom-call(s32[1,1,2,4,4]{4,3,2,1,0:T(4,128)} %pat.1, bf16[32,1024]{1,0:T(8,128)(2,1)} %bitcast.54, bf16[2,4,512,128]{3,2,1,0:T(8,128)(2,1)} %bitcast.53), custom_call_target="tpu_custom_call" | custom-call | flops 33554432 | bytes 1048576 | tf_op jit(solution)/shard_map/pallas_call | solution.py:149
  11.8 12.0 %all_to_all.10.parts = bf16[4,2,32,512]{3,2,1,0:T(8,128)(2,1)S(1)} all-to-all(bf16[4,2,32,512]{3,2,1,0:T(8,128)(2,1)} %shard_map.86), channel_id=1, replica_groups={{0,1,2,3},{4,5,6,7},{8,9,10,11},{12,13,14,15},{16,17,18,19},{20,21,22,2..., dimensions={0} | all-to-all | bytes 524288 | tf_op jit(solution)/shard_map/all_to_all | solution.py:138
  23.8 0.7 shard_map.87
  24.6 9.5 %all-to-all-start.1 = ((bf16[4,2,32,512]{3,2,1,0:T(8,128)(2,1)}), bf16[4,2,32,512]{3,2,1,0:T(8,128)(2,1)S(1)}, u32[]{:S(2)}, u32[]{:S(2)}) async-start(bf16[4,2,32,512]{3,2,1,0:T(8,128)(2,1)} %shard_map.87), calls=%async_computation.1 | async-start | bytes 524288 | tf_op jit(solution)/shard_map/all_to_all | solution.py:138
  34.0 0.1 reshape.38.pat
  34.2 15.4 %all-to-all-done.1.parts = bf16[4,2,32,512]{3,2,1,0:T(8,128)(2,1)S(1)} async-done(((bf16[4,2,32,512]{3,2,1,0:T(8,128)(2,1)}), bf16[4,2,32,512]{3,2,1,0:T(8,128)(2,1)S(1)}, u32[]{:S(2)}, u32[]{:S(2)}) %all-to-all-start.1) | async-done | bytes 262176 | tf_op jit(solution)/shard_map/all_to_all | solution.py:138
  49.6 5.5 %all-gather = bf16[2,1,32,512]{3,2,1,0:T(8,128)(2,1)S(1)} all-gather(bf16[1,1,32,512]{3,2,1,0:T(8,128)(2,1)S(1)} %fusion), channel_id=2, replica_groups=mesh['col'=16,'row'=2,'leaf'=16] {'row'}, dimensions={0}, use_global_device_ids=true | all-gather | bytes 98304 | tf_op jit(solution)/shard_map/all_gather | solution.py:187
  55.1 0.1 shard_map.89
  55.2 1.3 %collective-permute-start.2 = (bf16[2,32,512]{2,1,0:T(8,128)(2,1)S(1)}, bf16[2,32,512]{2,1,0:T(8,128)(2,1)S(1)}, u32[]{:S(2)}, u32[]{:S(2)}) collective-permute-start(bf16[2,32,512]{2,1,0:T(8,128)(2,1)S(1)} %get-tuple-element.31.refs_1_), channel_id=1, source_target_pairs={{96,128},{224,256},{352,384},{480,0},{97,129},{225,257},{353,385},... | collective-permute-start | bytes 196616 | tf_op jit(solution)/shard_map/ppermute | solution.py:221
  56.5 2.5 %shard_map.90 = (f32[32,512]{1,0:T(8,128)S(1)}, bf16[2,32,512]{2,1,0:T(8,128)(2,1)S(1)}, bf16[1024,1024]{1,0:T(8,128)(2,1)S(1)}, bf16[2,4,512,128]{3,2,1,0:T(8,128)(2,1)S(1)}) custom-call(bf16[2,32,512]{2,1,0:T(8,128)(2,1)S(1)} %bitcast.31, f32[2,32,512]{2,1,0:T(8,128)S(1)} %bitcast.29, s32[128]{0:T(128)S(1)} %reshape.38.pat, ...), custom_call_target="tpu_custom_call" | custom-call | flops 67108864 | bytes 3145728 | tf_op jit(solution)/shard_map/pallas_call | solution.py:192
  59.1 2.5 %collective-permute-start.1 = (bf16[2,32,512]{2,1,0:T(8,128)(2,1)S(1)}, bf16[2,32,512]{2,1,0:T(8,128)(2,1)S(1)}, u32[]{:S(2)}, u32[]{:S(2)}) collective-permute-start(bf16[2,32,512]{2,1,0:T(8,128)(2,1)S(1)} %get-tuple-element.33), channel_id=1, source_target_pairs={{0,32},{32,64},{64,96},{128,160},{160,192},{192,224},{256,288},{28... | collective-permute-start | bytes 196616 | tf_op jit(solution)/shard_map/ppermute | solution.py:221
  61.6 4.4 %collective-permute-done.2.carry = bf16[2,32,512]{2,1,0:T(8,128)(2,1)S(1)} collective-permute-done((bf16[2,32,512]{2,1,0:T(8,128)(2,1)S(1)}, bf16[2,32,512]{2,1,0:T(8,128)(2,1)S(1)}, u32[]{:S(2)}, u32[]{:S(2)}) %collective-permute-start.2) | collective-permute-done | bytes 65568 | tf_op jit(solution)/shard_map/ppermute | solution.py:221
  66.0 2.4 %all_gather.17.whole = bf16[2,32,512]{2,1,0:T(8,128)(2,1)S(1)} all-gather(bf16[1,32,512]{2,1,0:T(8,128)(2,1)S(1)} %fusion.3), channel_id=1, replica_groups=mesh['col'=16,'row'=2,'leaf'=16] {'row'}, dimensions={0}, use_global_device_ids=true | all-gather | bytes 98304 | tf_op jit(solution)/shard_map/all_gather | solution.py:187
  68.4 0.1 shard_map.91
  68.5 1.8 %shard_map.92 = (f32[32,512]{1,0:T(8,128)S(1)}, bf16[2,32,512]{2,1,0:T(8,128)(2,1)S(1)}, bf16[1024,1024]{1,0:T(8,128)(2,1)S(1)}, bf16[2,4,512,128]{3,2,1,0:T(8,128)(2,1)S(1)}) custom-call(bf16[2,32,512]{2,1,0:T(8,128)(2,1)S(1)} %all_gather.17.whole, bf16[2,32,512]{2,1,0:T(8,128)(2,1)S(1)} %collective-permute-done.2.carry, s32[128]{0:T(128)S(1)} %reshape.38.pat, ...), custom_call_target="tpu_custom_call" | custom-call | flops 67108864 | bytes 3145728 | tf_op jit(solution)/shard_map/pallas_call | solution.py:192
  70.3 1.3 %collective-permute-start.3 = (bf16[2,32,512]{2,1,0:T(8,128)(2,1)S(1)}, bf16[2,32,512]{2,1,0:T(8,128)(2,1)S(1)}, u32[]{:S(2)}, u32[]{:S(2)}) collective-permute-start(bf16[2,32,512]{2,1,0:T(8,128)(2,1)S(1)} %get-tuple-element.41), channel_id=1, source_target_pairs={{0,32},{32,64},{64,96},{128,160},{160,192},{192,224},{256,288},{28... | collective-permute-start | bytes 196616 | tf_op jit(solution)/shard_map/ppermute | solution.py:221
  71.6 1.3 %collective-permute-start.4 = (bf16[2,32,512]{2,1,0:T(8,128)(2,1)S(1)}, bf16[2,32,512]{2,1,0:T(8,128)(2,1)S(1)}, u32[]{:S(2)}, u32[]{:S(2)}) collective-permute-start(bf16[2,32,512]{2,1,0:T(8,128)(2,1)S(1)} %get-tuple-element.37.refs_1_), channel_id=1, source_target_pairs={{96,128},{224,256},{352,384},{480,0},{97,129},{225,257},{353,385},... | collective-permute-start | bytes 196616 | tf_op jit(solution)/shard_map/ppermute | solution.py:221
  72.9 7.0 %collective-permute-done.4.carry = bf16[2,32,512]{2,1,0:T(8,128)(2,1)S(1)} collective-permute-done((bf16[2,32,512]{2,1,0:T(8,128)(2,1)S(1)}, bf16[2,32,512]{2,1,0:T(8,128)(2,1)S(1)}, u32[]{:S(2)}, u32[]{:S(2)}) %collective-permute-start.4) | collective-permute-done | bytes 65568 | tf_op jit(solution)/shard_map/ppermute | solution.py:221
  80.0 3.2 %all_gather.18.whole = bf16[2,32,512]{2,1,0:T(8,128)(2,1)S(1)} all-gather(bf16[1,32,512]{2,1,0:T(8,128)(2,1)S(1)} %fusion.2), channel_id=1, replica_groups=mesh['col'=16,'row'=2,'leaf'=16] {'row'}, dimensions={0}, use_global_device_ids=true | all-gather | bytes 98304 | tf_op jit(solution)/shard_map/all_gather | solution.py:187
  83.3 1.8 %shard_map.94 = (f32[32,512]{1,0:T(8,128)S(1)}, bf16[2,32,512]{2,1,0:T(8,128)(2,1)S(1)}, bf16[1024,1024]{1,0:T(8,128)(2,1)S(1)}, bf16[2,4,512,128]{3,2,1,0:T(8,128)(2,1)S(1)}) custom-call(bf16[2,32,512]{2,1,0:T(8,128)(2,1)S(1)} %all_gather.18.whole, bf16[2,32,512]{2,1,0:T(8,128)(2,1)S(1)} %collective-permute-done.4.carry, s32[128]{0:T(128)S(1)} %reshape.38.pat, ...), custom_call_target="tpu_custom_call" | custom-call | flops 67108864 | bytes 3145728 | tf_op jit(solution)/shard_map/pallas_call | solution.py:192
  85.1 1.3 %collective-permute-start.5 = (bf16[2,32,512]{2,1,0:T(8,128)(2,1)S(1)}, bf16[2,32,512]{2,1,0:T(8,128)(2,1)S(1)}, u32[]{:S(2)}, u32[]{:S(2)}) collective-permute-start(bf16[2,32,512]{2,1,0:T(8,128)(2,1)S(1)} %get-tuple-element.49), channel_id=1, source_target_pairs={{0,32},{32,64},{64,96},{128,160},{160,192},{192,224},{256,288},{28... | collective-permute-start | bytes 196616 | tf_op jit(solution)/shard_map/ppermute | solution.py:221
  86.4 1.3 %collective-permute-start.6 = (bf16[2,32,512]{2,1,0:T(8,128)(2,1)S(1)}, bf16[2,32,512]{2,1,0:T(8,128)(2,1)S(1)}, u32[]{:S(2)}, u32[]{:S(2)}) collective-permute-start(bf16[2,32,512]{2,1,0:T(8,128)(2,1)S(1)} %get-tuple-element.45.refs_1_), channel_id=1, source_target_pairs={{96,128},{224,256},{352,384},{480,0},{97,129},{225,257},{353,385},... | collective-permute-start | bytes 196616 | tf_op jit(solution)/shard_map/ppermute | solution.py:221
  87.7 7.0 %collective-permute-done.6.carry = bf16[2,32,512]{2,1,0:T(8,128)(2,1)S(1)} collective-permute-done((bf16[2,32,512]{2,1,0:T(8,128)(2,1)S(1)}, bf16[2,32,512]{2,1,0:T(8,128)(2,1)S(1)}, u32[]{:S(2)}, u32[]{:S(2)}) %collective-permute-start.6) | collective-permute-done | bytes 65568 | tf_op jit(solution)/shard_map/ppermute | solution.py:221
  94.7 3.0 %all_gather.19.whole = bf16[2,32,512]{2,1,0:T(8,128)(2,1)S(1)} all-gather(bf16[1,32,512]{2,1,0:T(8,128)(2,1)S(1)} %fusion.1), channel_id=1, replica_groups=mesh['col'=16,'row'=2,'leaf'=16] {'row'}, dimensions={0}, use_global_device_ids=true | all-gather | bytes 98304 | tf_op jit(solution)/shard_map/all_gather | solution.py:187
  97.8 1.3 %collective-permute-start.8 = (bf16[2,32,512]{2,1,0:T(8,128)(2,1)S(1)}, bf16[2,32,512]{2,1,0:T(8,128)(2,1)S(1)}, u32[]{:S(2)}, u32[]{:S(2)}) collective-permute-start(bf16[2,32,512]{2,1,0:T(8,128)(2,1)S(1)} %get-tuple-element.53.refs_1_), channel_id=1, source_target_pairs={{96,128},{224,256},{352,384},{480,0},{97,129},{225,257},{353,385},... | collective-permute-start | bytes 196616 | tf_op jit(solution)/shard_map/ppermute | solution.py:221
  99.1 1.6 %shard_map.96 = (f32[32,512]{1,0:T(8,128)S(1)}, bf16[2,32,512]{2,1,0:T(8,128)(2,1)S(1)}) custom-call(bf16[2,32,512]{2,1,0:T(8,128)(2,1)S(1)} %all_gather.19.whole, bf16[2,32,512]{2,1,0:T(8,128)(2,1)S(1)} %collective-permute-done.6.carry, s32[128]{0:T(128)S(1)} %reshape.38.pat, bf16[4,512,1024]{2,1,0:T(8,128)(2,1)} %bitcast.44, ...), custom_call_target="tpu_custom_call" | custom-call | flops 67108864 | bytes 3145728 | tf_op jit(solution)/shard_map/pallas_call | solution.py:192
  100.8 1.3 %collective-permute-start.7 = (bf16[2,32,512]{2,1,0:T(8,128)(2,1)S(1)}, bf16[2,32,512]{2,1,0:T(8,128)(2,1)S(1)}, u32[]{:S(2)}, u32[]{:S(2)}) collective-permute-start(bf16[2,32,512]{2,1,0:T(8,128)(2,1)S(1)} %get-tuple-element.57), channel_id=1, source_target_pairs={{0,32},{32,64},{64,96},{128,160},{160,192},{192,224},{256,288},{28... | collective-permute-start | bytes 196616 | tf_op jit(solution)/shard_map/ppermute | solution.py:221
  102.1 0.7 maximum_bitcast_fusion
  102.8 0.6 collective-permute-done.7
  103.4 2.8 %collective-permute-done.8 = bf16[2,32,512]{2,1,0:T(8,128)(2,1)S(1)} collective-permute-done((bf16[2,32,512]{2,1,0:T(8,128)(2,1)S(1)}, bf16[2,32,512]{2,1,0:T(8,128)(2,1)S(1)}, u32[]{:S(2)}, u32[]{:S(2)}) %collective-permute-start.8) | collective-permute-done | bytes 65568 | tf_op jit(solution)/shard_map/ppermute | solution.py:221
  106.2 0.7 add_bitcast_fusion
  (15 shorter events, 0.3 us)
Async XLA Ops:
  0.6 33.4 %copy-start.1 = (s32[4,1,2,4,4]{4,3,2,1,0:T(4,128)S(1)}, s32[4,1,2,4,4]{4,3,2,1,0:T(4,128)}, u32[]{:S(2)}) copy-start(s32[4,1,2,4,4]{4,3,2,1,0:T(4,128)} %param.10) | copy-start | bytes 1540
  0.6 48.9 %copy-start = (f32[4,1,32,512]{3,2,1,0:T(8,128)S(1)}, f32[4,1,32,512]{3,2,1,0:T(8,128)}, u32[]{:S(2)}) copy-start(f32[4,1,32,512]{3,2,1,0:T(8,128)} %param.7) | copy-start | bytes 786436
  0.7 54.5 %collective-permute-start = (bf16[4,512,1024]{2,1,0:T(8,128)(2,1)}, bf16[4,512,1024]{2,1,0:T(8,128)(2,1)}, u32[]{:S(2)}, u32[]{:S(2)}) collective-permute-start(bf16[4,512,1024]{2,1,0:T(8,128)(2,1)} %bitcast.36), channel_id=1, source_target_pairs={{0,16},{16,0},{1,17},{17,1},{2,18},{18,2},{3,19},{19,3},{4,20},{20... | collective-permute-start | bytes 12582920 | tf_op jit(solution)/shard_map/ppermute | solution.py:173
  24.6 24.9 %all-to-all-start.1 = ((bf16[4,2,32,512]{3,2,1,0:T(8,128)(2,1)}), bf16[4,2,32,512]{3,2,1,0:T(8,128)(2,1)S(1)}, u32[]{:S(2)}, u32[]{:S(2)}) async-start(bf16[4,2,32,512]{3,2,1,0:T(8,128)(2,1)} %shard_map.87), calls=%async_computation.1 | async-start | bytes 524288 | tf_op jit(solution)/shard_map/all_to_all | solution.py:138
  55.2 10.7 %collective-permute-start.2 = (bf16[2,32,512]{2,1,0:T(8,128)(2,1)S(1)}, bf16[2,32,512]{2,1,0:T(8,128)(2,1)S(1)}, u32[]{:S(2)}, u32[]{:S(2)}) collective-permute-start(bf16[2,32,512]{2,1,0:T(8,128)(2,1)S(1)} %get-tuple-element.31.refs_1_), channel_id=1, source_target_pairs={{96,128},{224,256},{352,384},{480,0},{97,129},{225,257},{353,385},... | collective-permute-start | bytes 196616 | tf_op jit(solution)/shard_map/ppermute | solution.py:221
  59.1 6.9 %collective-permute-start.1 = (bf16[2,32,512]{2,1,0:T(8,128)(2,1)S(1)}, bf16[2,32,512]{2,1,0:T(8,128)(2,1)S(1)}, u32[]{:S(2)}, u32[]{:S(2)}) collective-permute-start(bf16[2,32,512]{2,1,0:T(8,128)(2,1)S(1)} %get-tuple-element.33), channel_id=1, source_target_pairs={{0,32},{32,64},{64,96},{128,160},{160,192},{192,224},{256,288},{28... | collective-permute-start | bytes 196616 | tf_op jit(solution)/shard_map/ppermute | solution.py:221
  70.3 2.6 %collective-permute-start.3 = (bf16[2,32,512]{2,1,0:T(8,128)(2,1)S(1)}, bf16[2,32,512]{2,1,0:T(8,128)(2,1)S(1)}, u32[]{:S(2)}, u32[]{:S(2)}) collective-permute-start(bf16[2,32,512]{2,1,0:T(8,128)(2,1)S(1)} %get-tuple-element.41), channel_id=1, source_target_pairs={{0,32},{32,64},{64,96},{128,160},{160,192},{192,224},{256,288},{28... | collective-permute-start | bytes 196616 | tf_op jit(solution)/shard_map/ppermute | solution.py:221
  71.6 8.3 %collective-permute-start.4 = (bf16[2,32,512]{2,1,0:T(8,128)(2,1)S(1)}, bf16[2,32,512]{2,1,0:T(8,128)(2,1)S(1)}, u32[]{:S(2)}, u32[]{:S(2)}) collective-permute-start(bf16[2,32,512]{2,1,0:T(8,128)(2,1)S(1)} %get-tuple-element.37.refs_1_), channel_id=1, source_target_pairs={{96,128},{224,256},{352,384},{480,0},{97,129},{225,257},{353,385},... | collective-permute-start | bytes 196616 | tf_op jit(solution)/shard_map/ppermute | solution.py:221
  85.1 2.6 %collective-permute-start.5 = (bf16[2,32,512]{2,1,0:T(8,128)(2,1)S(1)}, bf16[2,32,512]{2,1,0:T(8,128)(2,1)S(1)}, u32[]{:S(2)}, u32[]{:S(2)}) collective-permute-start(bf16[2,32,512]{2,1,0:T(8,128)(2,1)S(1)} %get-tuple-element.49), channel_id=1, source_target_pairs={{0,32},{32,64},{64,96},{128,160},{160,192},{192,224},{256,288},{28... | collective-permute-start | bytes 196616 | tf_op jit(solution)/shard_map/ppermute | solution.py:221
  86.4 8.3 %collective-permute-start.6 = (bf16[2,32,512]{2,1,0:T(8,128)(2,1)S(1)}, bf16[2,32,512]{2,1,0:T(8,128)(2,1)S(1)}, u32[]{:S(2)}, u32[]{:S(2)}) collective-permute-start(bf16[2,32,512]{2,1,0:T(8,128)(2,1)S(1)} %get-tuple-element.45.refs_1_), channel_id=1, source_target_pairs={{96,128},{224,256},{352,384},{480,0},{97,129},{225,257},{353,385},... | collective-permute-start | bytes 196616 | tf_op jit(solution)/shard_map/ppermute | solution.py:221
  97.8 8.3 %collective-permute-start.8 = (bf16[2,32,512]{2,1,0:T(8,128)(2,1)S(1)}, bf16[2,32,512]{2,1,0:T(8,128)(2,1)S(1)}, u32[]{:S(2)}, u32[]{:S(2)}) collective-permute-start(bf16[2,32,512]{2,1,0:T(8,128)(2,1)S(1)} %get-tuple-element.53.refs_1_), channel_id=1, source_target_pairs={{96,128},{224,256},{352,384},{480,0},{97,129},{225,257},{353,385},... | collective-permute-start | bytes 196616 | tf_op jit(solution)/shard_map/ppermute | solution.py:221
  100.8 2.6 %collective-permute-start.7 = (bf16[2,32,512]{2,1,0:T(8,128)(2,1)S(1)}, bf16[2,32,512]{2,1,0:T(8,128)(2,1)S(1)}, u32[]{:S(2)}, u32[]{:S(2)}) collective-permute-start(bf16[2,32,512]{2,1,0:T(8,128)(2,1)S(1)} %get-tuple-element.57), channel_id=1, source_target_pairs={{0,32},{32,64},{64,96},{128,160},{160,192},{192,224},{256,288},{28... | collective-permute-start | bytes 196616 | tf_op jit(solution)/shard_map/ppermute | solution.py:221

commit v2 on v1

--- a/solution.py
+++ b/solution.py
@@ -46,6 +46,14 @@
     total = total.astype(out.dtype)
     for copy in range(out.shape[0]):
         out[copy] = total
+
+
+def sum_kernel(*refs):
+    *parts, out = refs
+    total = parts[0][...].astype(F32)
+    for part in parts[1:]:
+        total = total + part[...].astype(F32)
+    out[...] = total
 
 
 def panel_copies(level, own, other, tiles, inverse, held, sems):
@@ -66,27 +74,27 @@
     return waits + [last.wait]
 
 
-def level_kernel(level, front, whole, carry, pat, own, other, tiles, *refs):
+def load_kernel(own, other, tiles, inverse, held, sems):
+    for wait in panel_copies(0, own, other, tiles, inverse, held, sems):
+        wait()
+
+
+def level_kernel(level, front, whole, carry, late, pat, own, other, tiles, *refs):
     refs = list(refs)
     passed = None if front else (refs.pop(0), refs.pop(0))
-    here = None if level == 0 else (refs.pop(0), refs.pop(0))
+    inverse, held = refs.pop(0), refs.pop(0)
     solved, send = refs.pop(0), refs.pop(0)
     ahead = (refs.pop(0), refs.pop(0)) if level < STEPS - 1 else None
-    blocks, picks, sems, ahead_sems = refs[:4]
+    blocks, picks, sem, ahead_sems = refs
     behind = lax.rem(lax.axis_index("col"), RING) == 0
 
     def work():
-        inverse, held = here or (refs[4], refs[5])
-        pattern = pltpu.make_async_copy(pat, picks, sems.at[5])
+        pattern = pltpu.make_async_copy(pat, picks, sem)
         pattern.start()
-        waits = [lambda: None] * 5
-        if here is None:
-            waits = panel_copies(level, own, other, tiles, inverse, held, sems)
         later = panel_copies(level + 1, own, other, tiles, *ahead, ahead_sems) if ahead else []
         me = lax.axis_index("row")
         rhs = jnp.concatenate([whole[0], whole[1]], axis=1)
         for part in range(4):
-            waits[part]()
             lo, width = part * 256, (part + 1) * 256
             x = dot(rhs[:, :width], inverse[lo : lo + 256, :width], 1)
             for q in range(2):
@@ -97,7 +105,6 @@
                 solved[:, (part % 2) * 256 : (part % 2) * 256 + 256] = x
 
         pattern.wait()
-        waits[4]()
         for h in range(2):
             for b in range(NB):
                 base = ((level * 2 + h) * NB + b) * NB
@@ -106,6 +113,8 @@
                 at = (slice(None), slice(b * BLK, (b + 1) * BLK))
                 if h == 0:
                     out = out + carry[(1, *at)].astype(F32)
+                    if level > 0:
+                        out = out + late[(1, *at)].astype(F32)
                 send[(h, *at)] = out.astype(BF16)
         for wait in later:
             wait()
@@ -145,7 +154,6 @@
     cols = lax.axis_size("col")
     state = (2, NRHS, HALF)
     near = [list(range(i, i + NEAR)) for i in range(0, leaves, NEAR)]
-    far = [list(range(i, leaves, NEAR)) for i in range(NEAR)]
     copies = call(
         subtree_kernel,
         jax.ShapeDtypeStruct((len(near[0]), *state), BF16),
@@ -154,21 +162,24 @@
         moved=1 << 20,
     )(sub_pattern, sub_solved[0, 0], sub_vals.reshape(2, NB, NB * BLK, BLK))
     arrived = exchange(copies, near)
-    copies = call(
+    part = call(
         merge_kernel,
-        jax.ShapeDtypeStruct((len(far[0]), *state), BF16),
+        jax.ShapeDtypeStruct((1, *state), BF16),
         [vmem],
         moved=1 << 19,
         limit=8 << 20,
     )(arrived)
-    arrived = exchange(copies, far)
+    parts = [part]
+    for d in (2 * NEAR, NEAR, 3 * NEAR):
+        route = [(i, (i + d) % leaves) for i in range(leaves)]
+        parts.append(lax.ppermute(part, "leaf", route))
     carry = call(
-        merge_kernel,
+        sum_kernel,
         jax.ShapeDtypeStruct((1, *state), F32),
-        [vmem],
+        [vmem] * len(parts),
         moved=1 << 19,
         limit=8 << 20,
-    )(arrived)[0]
+    )(*parts)[0]
     own = diag_inv[:, 0]
     other = lax.ppermute(own, "row", [(0, 1), (1, 0)])
     tiles = tile_vals[:, 0].reshape(STEPS, 2, NB, NB * BLK, BLK)
@@ -177,9 +188,19 @@
         jax.ShapeDtypeStruct((2, NB, NB * BLK, BLK), BF16),
     )
     pattern = tile_pattern.reshape(-1)
-    across = [(c, (c + 1) % cols) for c in range(RING - 1, cols, RING)]
-    along = [(c, c + 1) for c in range(cols) if c % RING != RING - 1]
-    solves, weights = [], {True: [], False: []}
+    moves = {
+        True: [(c, (c + 1) % cols) for c in range(cols) if c % RING],
+        False: [(c, c + 1) for c in range(0, cols, RING)],
+    }
+    loaded = call(
+        load_kernel,
+        panel,
+        [hbm, hbm, hbm],
+        [pltpu.SemaphoreType.DMA((5,))],
+        moved=3 << 20,
+        limit=EDGE << 20,
+    )(own, other, tiles)
+    solves, weights = [], {True: list(loaded), False: list(loaded)}
     carries = {True: carry, False: carry}
     for level in range(STEPS):
         total = carry[0] if level == 0 else carries[True][0] + carries[False][0]
@@ -196,20 +217,20 @@
                     jax.ShapeDtypeStruct(state, BF16),
                     *(() if last else panel),
                 ),
-                [vmem, vmem, hbm, hbm, hbm, hbm] + [vmem] * len(passed + weights[front]),
+                [vmem, vmem, vmem, hbm, hbm, hbm, hbm] + [vmem] * len(passed + weights[front]),
                 [
                     pltpu.VMEM((2 * NB, NRHS, BLK), BF16),
                     pltpu.SMEM(pattern.shape, jnp.int32),
-                    pltpu.SemaphoreType.DMA((6,)),
+                    pltpu.SemaphoreType.DMA,
                     pltpu.SemaphoreType.DMA((5,)),
-                    *(pltpu.VMEM(p.shape, p.dtype) for p in panel if level == 0),
                 ],
                 flops=2 * 32 * (1 << 20),
                 moved=3 << 20,
-                limit=(EDGE if level in (0, STEPS - 1) else LIMIT) << 20,
+                limit=(EDGE if last else LIMIT) << 20,
             )(
                 whole,
-                carries[front],
+                carries[True],
+                carries[False],
                 pattern,
                 own,
                 other,
@@ -218,7 +239,7 @@
                 *weights[front],
             )
             passed = [solved, send]
-            arrived[not front] = lax.ppermute(send, "col", across if front else along)
+            arrived[front] = lax.ppermute(send, "col", moves[front])
         solves.append(solved)
         carries = arrived
     outgoing = carries[True].astype(F32) + carries[False].astype(F32)

time: 108 us -> 108 us (level)
  starting transfers between devices: 29.9 us -> 40 us
  waiting for transfers between devices: 37.2 us -> 28 us
    ppermute x8 -> x11, starting transfers between devices: 11.5 us -> 31.1 us  [the longest x3 19.3 us: chain(): parts.append(lax.ppermute(part, 'leaf', route))]
    all_to_all x1 -> x0, waiting for transfers between devices: 15.4 us -> none  [exchange(): lax.all_to_all(parts, 'leaf', split_axis=0, concat_axis=0, tiled=True, ax...]
    all_to_all x1 -> x0, starting transfers between devices: 9.46 us -> none  [exchange(): lax.all_to_all(parts, 'leaf', split_axis=0, concat_axis=0, tiled=True, ax...]
    ppermute x8 -> x11, waiting for transfers between devices: 21.8 us -> 28 us  [the longest x8 24.5 us: chain(): arrived[front] = lax.ppermute(send, 'col', moves[front])]
    pallas_call x8, Pallas kernels: 8.14 us -> 7.06 us  [chain(): call(functools.partial(level_kernel, level, front), (jax.ShapeDtypeStruct...]
  transfers between devices with their start and end apart: 10 -> 12, of which waited for: 6 -> 6; matrix products, arithmetic and copies ran while one was open for 1% -> 1% of each run, Pallas kernels for 7% -> 4%
where the time goes in v2:
time: 108 us; the launch traced here: 107 us
  starting transfers between devices  40 us (37%)
  waiting for transfers between devices  28 us (26%)
  blocking collectives  25.8 us (24%)
  Pallas kernels  11.1 us (10%)
  other arithmetic  1.45 us (1%)
    ppermute x8, waiting for transfers between devices, chain(): arrived[front] = lax.ppermute(send, 'col', moves[front])  24.5 us
    ppermute x3, starting transfers between devices, chain(): parts.append(lax.ppermute(part, 'leaf', route))  19.3 us
    all_gather x4, blocking collectives, chain(): whole = lax.all_gather(rhs, 'row', axis=0, tiled=False)  13.7 us
    all_to_all x1, blocking collectives, exchange(): lax.all_to_all(parts, 'leaf', split_axis=0, concat_axis=0, tiled=True, ax...  12 us
    ppermute x8, starting transfers between devices, chain(): arrived[front] = lax.ppermute(send, 'col', moves[front])  11.8 us
    ppermute x1, starting transfers between devices, chain(): other = lax.ppermute(own, 'row', [(0, 1), (1, 0)])  8.88 us
    pallas_call x8, Pallas kernels, chain(): call(functools.partial(level_kernel, level, front), (jax.ShapeDtypeStruct...  7.06 us
    ppermute x3, waiting for transfers between devices, chain(): parts.append(lax.ppermute(part, 'leaf', route))  3.54 us
  transfers between devices with their start and end apart: 12, of which 6 were waited for; matrix products, arithmetic and copies ran while one was open for 1% of the time, Pallas kernels for 4%

profile of v2, /device:TPU:1, one launch (start us, length us, event | category | flops | bytes accessed | tf_op | source)
XLA Modules:
  0.0 107.3 jit_solution(18171837935593127911)
XLA Ops:
  0.7 8.9 %collective-permute-start.3 = (bf16[4,512,1024]{2,1,0:T(8,128)(2,1)}, bf16[4,512,1024]{2,1,0:T(8,128)(2,1)}, u32[]{:S(2)}, u32[]{:S(2)}) collective-permute-start(bf16[4,512,1024]{2,1,0:T(8,128)(2,1)} %bitcast.38), channel_id=1, source_target_pairs={{0,16},{16,0},{1,17},{17,1},{2,18},{18,2},{3,19},{19,3},{4,20},{20... | collective-permute-start | bytes 12582920 | tf_op jit(solution)/shard_map/ppermute | solution.py:184
  9.5 2.3 %shard_map.86 = bf16[4,2,32,512]{3,2,1,0:T(8,128)(2,1)} custom-call(s32[1,1,2,4,4]{4,3,2,1,0:T(4,128)} %pat.1, bf16[32,1024]{1,0:T(8,128)(2,1)} %bitcast.58, bf16[2,4,512,128]{3,2,1,0:T(8,128)(2,1)} %bitcast.57), custom_call_target="tpu_custom_call" | custom-call | flops 33554432 | bytes 1048576 | tf_op jit(solution)/shard_map/pallas_call | solution.py:157
  11.8 12.0 %all_to_all.5.parts = bf16[4,2,32,512]{3,2,1,0:T(8,128)(2,1)S(1)} all-to-all(bf16[4,2,32,512]{3,2,1,0:T(8,128)(2,1)} %shard_map.86), channel_id=1, replica_groups={{0,1,2,3},{4,5,6,7},{8,9,10,11},{12,13,14,15},{16,17,18,19},{20,21,22,2..., dimensions={0} | all-to-all | bytes 524288 | tf_op jit(solution)/shard_map/all_to_all | solution.py:147
  23.9 7.1 %collective-permute-start.2 = (bf16[1,2,32,512]{3,2,1,0:T(8,128)(2,1)S(1)}, bf16[1,2,32,512]{3,2,1,0:T(8,128)(2,1)S(1)}, u32[]{:S(2)}, u32[]{:S(2)}) collective-permute-start(bf16[1,2,32,512]{3,2,1,0:T(8,128)(2,1)S(1)} %shard_map.87.refs_0_), channel_id=1, source_target_pairs={{0,12},{1,13},{2,14},{3,15},{4,0},{5,1},{6,2},{7,3},{8,4},{9,5},{1... | collective-permute-start | bytes 196616 | tf_op jit(solution)/shard_map/ppermute | solution.py:175
  31.0 2.1 %collective-permute-start.1 = (bf16[1,2,32,512]{3,2,1,0:T(8,128)(2,1)S(1)}, bf16[1,2,32,512]{3,2,1,0:T(8,128)(2,1)S(1)}, u32[]{:S(2)}, u32[]{:S(2)}) collective-permute-start(bf16[1,2,32,512]{3,2,1,0:T(8,128)(2,1)S(1)} %shard_map.87.refs_0_), channel_id=1, source_target_pairs={{0,4},{1,5},{2,6},{3,7},{4,8},{5,9},{6,10},{7,11},{8,12},{9,13},{1... | collective-permute-start | bytes 196616 | tf_op jit(solution)/shard_map/ppermute | solution.py:175
  33.1 10.1 %collective-permute-start = (bf16[1,2,32,512]{3,2,1,0:T(8,128)(2,1)S(1)}, bf16[1,2,32,512]{3,2,1,0:T(8,128)(2,1)S(1)}, u32[]{:S(2)}, u32[]{:S(2)}) collective-permute-start(bf16[1,2,32,512]{3,2,1,0:T(8,128)(2,1)S(1)} %shard_map.87.refs_0_), channel_id=1, source_target_pairs={{0,8},{1,9},{2,10},{3,11},{4,12},{5,13},{6,14},{7,15},{8,0},{9,1},... | collective-permute-start | bytes 196616 | tf_op jit(solution)/shard_map/ppermute | solution.py:175
  43.2 0.1 reshape.38.pat
  43.3 3.5 %collective-permute-done.refs_1_ = bf16[1,2,32,512]{3,2,1,0:T(8,128)(2,1)S(1)} collective-permute-done((bf16[1,2,32,512]{3,2,1,0:T(8,128)(2,1)S(1)}, bf16[1,2,32,512]{3,2,1,0:T(8,128)(2,1)S(1)}, u32[]{:S(2)}, u32[]{:S(2)}) %collective-permute-start) | collective-permute-done | bytes 65568 | tf_op jit(solution)/shard_map/ppermute | solution.py:175
  46.9 4.4 %all-gather = bf16[2,1,32,512]{3,2,1,0:T(8,128)(2,1)S(1)} all-gather(bf16[1,1,32,512]{3,2,1,0:T(8,128)(2,1)S(1)} %fusion), channel_id=2, replica_groups=mesh['col'=16,'row'=2,'leaf'=16] {'row'}, dimensions={0}, use_global_device_ids=true | all-gather | bytes 98304 | tf_op jit(solution)/shard_map/all_gather | solution.py:208
  51.4 1.7 %shard_map.89 = (bf16[1024,1024]{1,0:T(8,128)(2,1)S(1)}, bf16[2,4,512,128]{3,2,1,0:T(8,128)(2,1)S(1)}) custom-call(bf16[4,512,1024]{2,1,0:T(8,128)(2,1)} %bitcast.39, bf16[4,512,1024]{2,1,0:T(8,128)(2,1)} %collective-permute-done.3.other, bf16[4,2,4,512,128]{4,3,2,1,0:T(8,128)(2,1)} %bitcast.48), custom_call_target="tpu_custom_call" | custom-call | bytes 3145728 | tf_op jit(solution)/shard_map/pallas_call | solution.py:195
  53.2 1.7 %shard_map.91 = (f32[32,512]{1,0:T(8,128)S(1)}, bf16[2,32,512]{2,1,0:T(8,128)(2,1)S(1)}, bf16[1024,1024]{1,0:T(8,128)(2,1)S(1)}, bf16[2,4,512,128]{3,2,1,0:T(8,128)(2,1)S(1)}) custom-call(bf16[2,32,512]{2,1,0:T(8,128)(2,1)S(1)} %bitcast.33, f32[2,32,512]{2,1,0:T(8,128)S(1)} %bitcast.30, f32[2,32,512]{2,1,0:T(8,128)S(1)} %bitcast.31, s32[128]{0:T(128)S(1)} %reshape.38.pat, ...), custom_call_target="tpu_custom_call" | custom-call | flops 67108864 | bytes 3145728 | tf_op jit(solution)/shard_map/pallas_call | solution.py:213
  54.9 2.8 %collective-permute-start.5 = (bf16[2,32,512]{2,1,0:T(8,128)(2,1)S(1)}, bf16[2,32,512]{2,1,0:T(8,128)(2,1)S(1)}, u32[]{:S(2)}, u32[]{:S(2)}) collective-permute-start(bf16[2,32,512]{2,1,0:T(8,128)(2,1)S(1)} %get-tuple-element.37), channel_id=1, source_target_pairs={{0,32},{128,160},{256,288},{384,416},{1,33},{129,161},{257,289},{3... | collective-permute-start | bytes 196616 | tf_op jit(solution)/shard_map/ppermute | solution.py:242
  57.7 1.3 %collective-permute-start.4 = (bf16[2,32,512]{2,1,0:T(8,128)(2,1)S(1)}, bf16[2,32,512]{2,1,0:T(8,128)(2,1)S(1)}, u32[]{:S(2)}, u32[]{:S(2)}) collective-permute-start(bf16[2,32,512]{2,1,0:T(8,128)(2,1)S(1)} %get-tuple-element.35.refs_1_), channel_id=1, source_target_pairs={{32,64},{64,96},{96,128},{160,192},{192,224},{224,256},{288,320},{... | collective-permute-start | bytes 196616 | tf_op jit(solution)/shard_map/ppermute | solution.py:242
  59.0 7.0 %collective-permute-done.4.carry = bf16[2,32,512]{2,1,0:T(8,128)(2,1)S(1)} collective-permute-done((bf16[2,32,512]{2,1,0:T(8,128)(2,1)S(1)}, bf16[2,32,512]{2,1,0:T(8,128)(2,1)S(1)}, u32[]{:S(2)}, u32[]{:S(2)}) %collective-permute-start.4) | collective-permute-done | bytes 65568 | tf_op jit(solution)/shard_map/ppermute | solution.py:242
  66.1 3.3 %all_gather.17.whole = bf16[2,32,512]{2,1,0:T(8,128)(2,1)S(1)} all-gather(bf16[1,32,512]{2,1,0:T(8,128)(2,1)S(1)} %fusion.3), channel_id=1, replica_groups=mesh['col'=16,'row'=2,'leaf'=16] {'row'}, dimensions={0}, use_global_device_ids=true | all-gather | bytes 98304 | tf_op jit(solution)/shard_map/all_gather | solution.py:208
  69.4 1.7 %shard_map.93 = (f32[32,512]{1,0:T(8,128)S(1)}, bf16[2,32,512]{2,1,0:T(8,128)(2,1)S(1)}, bf16[1024,1024]{1,0:T(8,128)(2,1)S(1)}, bf16[2,4,512,128]{3,2,1,0:T(8,128)(2,1)S(1)}) custom-call(bf16[2,32,512]{2,1,0:T(8,128)(2,1)S(1)} %all_gather.17.whole, bf16[2,32,512]{2,1,0:T(8,128)(2,1)S(1)} %collective-permute-done.4.carry, ...), custom_call_target="tpu_custom_call" | custom-call | flops 67108864 | bytes 3145728 | tf_op jit(solution)/shard_map/pallas_call | solution.py:213
  71.2 1.3 %collective-permute-start.7 = (bf16[2,32,512]{2,1,0:T(8,128)(2,1)S(1)}, bf16[2,32,512]{2,1,0:T(8,128)(2,1)S(1)}, u32[]{:S(2)}, u32[]{:S(2)}) collective-permute-start(bf16[2,32,512]{2,1,0:T(8,128)(2,1)S(1)} %get-tuple-element.45), channel_id=1, source_target_pairs={{0,32},{128,160},{256,288},{384,416},{1,33},{129,161},{257,289},{3... | collective-permute-start | bytes 196616 | tf_op jit(solution)/shard_map/ppermute | solution.py:242
  72.5 1.3 %collective-permute-start.6 = (bf16[2,32,512]{2,1,0:T(8,128)(2,1)S(1)}, bf16[2,32,512]{2,1,0:T(8,128)(2,1)S(1)}, u32[]{:S(2)}, u32[]{:S(2)}) collective-permute-start(bf16[2,32,512]{2,1,0:T(8,128)(2,1)S(1)} %get-tuple-element.41.refs_1_), channel_id=1, source_target_pairs={{32,64},{64,96},{96,128},{160,192},{192,224},{224,256},{288,320},{... | collective-permute-start | bytes 196616 | tf_op jit(solution)/shard_map/ppermute | solution.py:242
  73.8 7.0 %collective-permute-done.6.carry = bf16[2,32,512]{2,1,0:T(8,128)(2,1)S(1)} collective-permute-done((bf16[2,32,512]{2,1,0:T(8,128)(2,1)S(1)}, bf16[2,32,512]{2,1,0:T(8,128)(2,1)S(1)}, u32[]{:S(2)}, u32[]{:S(2)}) %collective-permute-start.6) | collective-permute-done | bytes 65568 | tf_op jit(solution)/shard_map/ppermute | solution.py:242
  80.8 3.0 %all_gather.18.whole = bf16[2,32,512]{2,1,0:T(8,128)(2,1)S(1)} all-gather(bf16[1,32,512]{2,1,0:T(8,128)(2,1)S(1)} %fusion.2), channel_id=1, replica_groups=mesh['col'=16,'row'=2,'leaf'=16] {'row'}, dimensions={0}, use_global_device_ids=true | all-gather | bytes 98304 | tf_op jit(solution)/shard_map/all_gather | solution.py:208
  83.9 1.7 %shard_map.95 = (f32[32,512]{1,0:T(8,128)S(1)}, bf16[2,32,512]{2,1,0:T(8,128)(2,1)S(1)}, bf16[1024,1024]{1,0:T(8,128)(2,1)S(1)}, bf16[2,4,512,128]{3,2,1,0:T(8,128)(2,1)S(1)}) custom-call(bf16[2,32,512]{2,1,0:T(8,128)(2,1)S(1)} %all_gather.18.whole, bf16[2,32,512]{2,1,0:T(8,128)(2,1)S(1)} %collective-permute-done.6.carry, ...), custom_call_target="tpu_custom_call" | custom-call | flops 67108864 | bytes 3145728 | tf_op jit(solution)/shard_map/pallas_call | solution.py:213
  85.6 1.3 %collective-permute-start.9 = (bf16[2,32,512]{2,1,0:T(8,128)(2,1)S(1)}, bf16[2,32,512]{2,1,0:T(8,128)(2,1)S(1)}, u32[]{:S(2)}, u32[]{:S(2)}) collective-permute-start(bf16[2,32,512]{2,1,0:T(8,128)(2,1)S(1)} %get-tuple-element.53), channel_id=1, source_target_pairs={{0,32},{128,160},{256,288},{384,416},{1,33},{129,161},{257,289},{3... | collective-permute-start | bytes 196616 | tf_op jit(solution)/shard_map/ppermute | solution.py:242
  86.9 1.3 %collective-permute-start.8 = (bf16[2,32,512]{2,1,0:T(8,128)(2,1)S(1)}, bf16[2,32,512]{2,1,0:T(8,128)(2,1)S(1)}, u32[]{:S(2)}, u32[]{:S(2)}) collective-permute-start(bf16[2,32,512]{2,1,0:T(8,128)(2,1)S(1)} %get-tuple-element.49.refs_1_), channel_id=1, source_target_pairs={{32,64},{64,96},{96,128},{160,192},{192,224},{224,256},{288,320},{... | collective-permute-start | bytes 196616 | tf_op jit(solution)/shard_map/ppermute | solution.py:242
  88.2 7.0 %collective-permute-done.8.carry = bf16[2,32,512]{2,1,0:T(8,128)(2,1)S(1)} collective-permute-done((bf16[2,32,512]{2,1,0:T(8,128)(2,1)S(1)}, bf16[2,32,512]{2,1,0:T(8,128)(2,1)S(1)}, u32[]{:S(2)}, u32[]{:S(2)}) %collective-permute-start.8) | collective-permute-done | bytes 65568 | tf_op jit(solution)/shard_map/ppermute | solution.py:242
  95.3 3.0 %all_gather.19.whole = bf16[2,32,512]{2,1,0:T(8,128)(2,1)S(1)} all-gather(bf16[1,32,512]{2,1,0:T(8,128)(2,1)S(1)} %fusion.1), channel_id=1, replica_groups=mesh['col'=16,'row'=2,'leaf'=16] {'row'}, dimensions={0}, use_global_device_ids=true | all-gather | bytes 98304 | tf_op jit(solution)/shard_map/all_gather | solution.py:208
  98.3 1.3 %collective-permute-start.10 = (bf16[2,32,512]{2,1,0:T(8,128)(2,1)S(1)}, bf16[2,32,512]{2,1,0:T(8,128)(2,1)S(1)}, u32[]{:S(2)}, u32[]{:S(2)}) collective-permute-start(bf16[2,32,512]{2,1,0:T(8,128)(2,1)S(1)} %get-tuple-element.57.refs_1_), channel_id=1, source_target_pairs={{32,64},{64,96},{96,128},{160,192},{192,224},{224,256},{288,320},{... | collective-permute-start | bytes 196616 | tf_op jit(solution)/shard_map/ppermute | solution.py:242
  99.6 1.6 %shard_map.97 = (f32[32,512]{1,0:T(8,128)S(1)}, bf16[2,32,512]{2,1,0:T(8,128)(2,1)S(1)}) custom-call(bf16[2,32,512]{2,1,0:T(8,128)(2,1)S(1)} %all_gather.19.whole, bf16[2,32,512]{2,1,0:T(8,128)(2,1)S(1)} %collective-permute-done.8.carry, bf16[2,32,512]{2,1,0:T(8,128)(2,1)S(1)} %collective-permute-done.9.late, s32[128]{0:T(128)S(1)} %reshape.38.pat, ...), custom_call_target="tpu_custom_call" | custom-call | flops 67108864 | bytes 3145728 | tf_op jit(solution)/shard_map/pallas_call | solution.py:213
  101.2 1.3 %collective-permute-start.11 = (bf16[2,32,512]{2,1,0:T(8,128)(2,1)S(1)}, bf16[2,32,512]{2,1,0:T(8,128)(2,1)S(1)}, u32[]{:S(2)}, u32[]{:S(2)}) collective-permute-start(bf16[2,32,512]{2,1,0:T(8,128)(2,1)S(1)} %get-tuple-element.61), channel_id=1, source_target_pairs={{0,32},{128,160},{256,288},{384,416},{1,33},{129,161},{257,289},{3... | collective-permute-start | bytes 196616 | tf_op jit(solution)/shard_map/ppermute | solution.py:242
  102.5 0.7 maximum_bitcast_fusion
  103.3 0.6 collective-permute-done.11
  103.8 2.8 %collective-permute-done.10 = bf16[2,32,512]{2,1,0:T(8,128)(2,1)S(1)} collective-permute-done((bf16[2,32,512]{2,1,0:T(8,128)(2,1)S(1)}, bf16[2,32,512]{2,1,0:T(8,128)(2,1)S(1)}, u32[]{:S(2)}, u32[]{:S(2)}) %collective-permute-start.10) | collective-permute-done | bytes 65568 | tf_op jit(solution)/shard_map/ppermute | solution.py:242
  106.7 0.7 add_bitcast_fusion
  (20 shorter events, 0.4 us)
Async XLA Ops:
  0.6 42.6 %copy-start.1 = (s32[4,1,2,4,4]{4,3,2,1,0:T(4,128)S(1)}, s32[4,1,2,4,4]{4,3,2,1,0:T(4,128)}, u32[]{:S(2)}) copy-start(s32[4,1,2,4,4]{4,3,2,1,0:T(4,128)} %param.10) | copy-start | bytes 1540
  0.6 46.3 %copy-start = (f32[4,1,32,512]{3,2,1,0:T(8,128)S(1)}, f32[4,1,32,512]{3,2,1,0:T(8,128)}, u32[]{:S(2)}) copy-start(f32[4,1,32,512]{3,2,1,0:T(8,128)} %param.7) | copy-start | bytes 786436
  0.7 50.7 %collective-permute-start.3 = (bf16[4,512,1024]{2,1,0:T(8,128)(2,1)}, bf16[4,512,1024]{2,1,0:T(8,128)(2,1)}, u32[]{:S(2)}, u32[]{:S(2)}) collective-permute-start(bf16[4,512,1024]{2,1,0:T(8,128)(2,1)} %bitcast.38), channel_id=1, source_target_pairs={{0,16},{16,0},{1,17},{17,1},{2,18},{18,2},{3,19},{19,3},{4,20},{20... | collective-permute-start | bytes 12582920 | tf_op jit(solution)/shard_map/ppermute | solution.py:184
  23.9 19.4 %collective-permute-start.2 = (bf16[1,2,32,512]{3,2,1,0:T(8,128)(2,1)S(1)}, bf16[1,2,32,512]{3,2,1,0:T(8,128)(2,1)S(1)}, u32[]{:S(2)}, u32[]{:S(2)}) collective-permute-start(bf16[1,2,32,512]{3,2,1,0:T(8,128)(2,1)S(1)} %shard_map.87.refs_0_), channel_id=1, source_target_pairs={{0,12},{1,13},{2,14},{3,15},{4,0},{5,1},{6,2},{7,3},{8,4},{9,5},{1... | collective-permute-start | bytes 196616 | tf_op jit(solution)/shard_map/ppermute | solution.py:175
  31.0 12.3 %collective-permute-start.1 = (bf16[1,2,32,512]{3,2,1,0:T(8,128)(2,1)S(1)}, bf16[1,2,32,512]{3,2,1,0:T(8,128)(2,1)S(1)}, u32[]{:S(2)}, u32[]{:S(2)}) collective-permute-start(bf16[1,2,32,512]{3,2,1,0:T(8,128)(2,1)S(1)} %shard_map.87.refs_0_), channel_id=1, source_target_pairs={{0,4},{1,5},{2,6},{3,7},{4,8},{5,9},{6,10},{7,11},{8,12},{9,13},{1... | collective-permute-start | bytes 196616 | tf_op jit(solution)/shard_map/ppermute | solution.py:175
  33.1 13.8 %collective-permute-start = (bf16[1,2,32,512]{3,2,1,0:T(8,128)(2,1)S(1)}, bf16[1,2,32,512]{3,2,1,0:T(8,128)(2,1)S(1)}, u32[]{:S(2)}, u32[]{:S(2)}) collective-permute-start(bf16[1,2,32,512]{3,2,1,0:T(8,128)(2,1)S(1)} %shard_map.87.refs_0_), channel_id=1, source_target_pairs={{0,8},{1,9},{2,10},{3,11},{4,12},{5,13},{6,14},{7,15},{8,0},{9,1},... | collective-permute-start | bytes 196616 | tf_op jit(solution)/shard_map/ppermute | solution.py:175
  54.9 4.1 %collective-permute-start.5 = (bf16[2,32,512]{2,1,0:T(8,128)(2,1)S(1)}, bf16[2,32,512]{2,1,0:T(8,128)(2,1)S(1)}, u32[]{:S(2)}, u32[]{:S(2)}) collective-permute-start(bf16[2,32,512]{2,1,0:T(8,128)(2,1)S(1)} %get-tuple-element.37), channel_id=1, source_target_pairs={{0,32},{128,160},{256,288},{384,416},{1,33},{129,161},{257,289},{3... | collective-permute-start | bytes 196616 | tf_op jit(solution)/shard_map/ppermute | solution.py:242
  57.7 8.3 %collective-permute-start.4 = (bf16[2,32,512]{2,1,0:T(8,128)(2,1)S(1)}, bf16[2,32,512]{2,1,0:T(8,128)(2,1)S(1)}, u32[]{:S(2)}, u32[]{:S(2)}) collective-permute-start(bf16[2,32,512]{2,1,0:T(8,128)(2,1)S(1)} %get-tuple-element.35.refs_1_), channel_id=1, source_target_pairs={{32,64},{64,96},{96,128},{160,192},{192,224},{224,256},{288,320},{... | collective-permute-start | bytes 196616 | tf_op jit(solution)/shard_map/ppermute | solution.py:242
  71.2 2.6 %collective-permute-start.7 = (bf16[2,32,512]{2,1,0:T(8,128)(2,1)S(1)}, bf16[2,32,512]{2,1,0:T(8,128)(2,1)S(1)}, u32[]{:S(2)}, u32[]{:S(2)}) collective-permute-start(bf16[2,32,512]{2,1,0:T(8,128)(2,1)S(1)} %get-tuple-element.45), channel_id=1, source_target_pairs={{0,32},{128,160},{256,288},{384,416},{1,33},{129,161},{257,289},{3... | collective-permute-start | bytes 196616 | tf_op jit(solution)/shard_map/ppermute | solution.py:242
  72.5 8.3 %collective-permute-start.6 = (bf16[2,32,512]{2,1,0:T(8,128)(2,1)S(1)}, bf16[2,32,512]{2,1,0:T(8,128)(2,1)S(1)}, u32[]{:S(2)}, u32[]{:S(2)}) collective-permute-start(bf16[2,32,512]{2,1,0:T(8,128)(2,1)S(1)} %get-tuple-element.41.refs_1_), channel_id=1, source_target_pairs={{32,64},{64,96},{96,128},{160,192},{192,224},{224,256},{288,320},{... | collective-permute-start | bytes 196616 | tf_op jit(solution)/shard_map/ppermute | solution.py:242
  85.6 2.6 %collective-permute-start.9 = (bf16[2,32,512]{2,1,0:T(8,128)(2,1)S(1)}, bf16[2,32,512]{2,1,0:T(8,128)(2,1)S(1)}, u32[]{:S(2)}, u32[]{:S(2)}) collective-permute-start(bf16[2,32,512]{2,1,0:T(8,128)(2,1)S(1)} %get-tuple-element.53), channel_id=1, source_target_pairs={{0,32},{128,160},{256,288},{384,416},{1,33},{129,161},{257,289},{3... | collective-permute-start | bytes 196616 | tf_op jit(solution)/shard_map/ppermute | solution.py:242
  86.9 8.3 %collective-permute-start.8 = (bf16[2,32,512]{2,1,0:T(8,128)(2,1)S(1)}, bf16[2,32,512]{2,1,0:T(8,128)(2,1)S(1)}, u32[]{:S(2)}, u32[]{:S(2)}) collective-permute-start(bf16[2,32,512]{2,1,0:T(8,128)(2,1)S(1)} %get-tuple-element.49.refs_1_), channel_id=1, source_target_pairs={{32,64},{64,96},{96,128},{160,192},{192,224},{224,256},{288,320},{... | collective-permute-start | bytes 196616 | tf_op jit(solution)/shard_map/ppermute | solution.py:242
  98.3 8.3 %collective-permute-start.10 = (bf16[2,32,512]{2,1,0:T(8,128)(2,1)S(1)}, bf16[2,32,512]{2,1,0:T(8,128)(2,1)S(1)}, u32[]{:S(2)}, u32[]{:S(2)}) collective-permute-start(bf16[2,32,512]{2,1,0:T(8,128)(2,1)S(1)} %get-tuple-element.57.refs_1_), channel_id=1, source_target_pairs={{32,64},{64,96},{96,128},{160,192},{192,224},{224,256},{288,320},{... | collective-permute-start | bytes 196616 | tf_op jit(solution)/shard_map/ppermute | solution.py:242
  101.2 2.6 %collective-permute-start.11 = (bf16[2,32,512]{2,1,0:T(8,128)(2,1)S(1)}, bf16[2,32,512]{2,1,0:T(8,128)(2,1)S(1)}, u32[]{:S(2)}, u32[]{:S(2)}) collective-permute-start(bf16[2,32,512]{2,1,0:T(8,128)(2,1)S(1)} %get-tuple-element.61), channel_id=1, source_target_pairs={{0,32},{128,160},{256,288},{384,416},{1,33},{129,161},{257,289},{3... | collective-permute-start | bytes 196616 | tf_op jit(solution)/shard_map/ppermute | solution.py:242

commit v3 on v2

--- a/solution.py
+++ b/solution.py
@@ -14,7 +14,6 @@
 HALF = NB * BLK
 NRHS = 32
 NEAR = 4
-RING = 4
 LIMIT = 44
 EDGE = 48
 F32 = jnp.float32
@@ -86,7 +85,7 @@
     solved, send = refs.pop(0), refs.pop(0)
     ahead = (refs.pop(0), refs.pop(0)) if level < STEPS - 1 else None
     blocks, picks, sem, ahead_sems = refs
-    behind = lax.rem(lax.axis_index("col"), RING) == 0
+    behind = lax.rem(lax.axis_index("col"), 2) == 0
 
     def work():
         pattern = pltpu.make_async_copy(pat, picks, sem)
@@ -189,8 +188,8 @@
     )
     pattern = tile_pattern.reshape(-1)
     moves = {
-        True: [(c, (c + 1) % cols) for c in range(cols) if c % RING],
-        False: [(c, c + 1) for c in range(0, cols, RING)],
+        True: [(c, (c + 1) % cols) for c in range(cols) if c % 2],
+        False: [(c, (c + 1) % cols) for c in range(cols) if not (c % 2)],
     }
     loaded = call(
         load_kernel,

time: 108 us -> 108 us (level)
  no operation moved by 1% of the time
where the time goes in v3:
time: 108 us; the launch traced here: 107 us
  starting transfers between devices  40 us (37%)
  waiting for transfers between devices  28 us (26%)
  blocking collectives  25.8 us (24%)
  Pallas kernels  11.1 us (10%)
  other arithmetic  1.45 us (1%)
    ppermute x8, waiting for transfers between devices, chain(): arrived[front] = lax.ppermute(send, 'col', moves[front])  24.5 us
    ppermute x3, starting transfers between devices, chain(): parts.append(lax.ppermute(part, 'leaf', route))  19.3 us
    all_gather x4, blocking collectives, chain(): whole = lax.all_gather(rhs, 'row', axis=0, tiled=False)  13.7 us
    all_to_all x1, blocking collectives, exchange(): lax.all_to_all(parts, 'leaf', split_axis=0, concat_axis=0, tiled=True, ax...  12 us
    ppermute x8, starting transfers between devices, chain(): arrived[front] = lax.ppermute(send, 'col', moves[front])  11.8 us
    ppermute x1, starting transfers between devices, chain(): other = lax.ppermute(own, 'row', [(0, 1), (1, 0)])  8.88 us
    pallas_call x8, Pallas kernels, chain(): call(functools.partial(level_kernel, level, front), (jax.ShapeDtypeStruct...  7.06 us
    ppermute x3, waiting for transfers between devices, chain(): parts.append(lax.ppermute(part, 'leaf', route))  3.54 us
  transfers between devices with their start and end apart: 12, of which 6 were waited for; matrix products, arithmetic and copies ran while one was open for 1% of the time, Pallas kernels for 4%

profile of v3, /device:TPU:1, one launch (start us, length us, event | category | flops | bytes accessed | tf_op | source)
XLA Modules:
  0.0 107.3 jit_solution(10796234620233037937)
XLA Ops:
  0.7 8.9 %collective-permute-start.3 = (bf16[4,512,1024]{2,1,0:T(8,128)(2,1)}, bf16[4,512,1024]{2,1,0:T(8,128)(2,1)}, u32[]{:S(2)}, u32[]{:S(2)}) collective-permute-start(bf16[4,512,1024]{2,1,0:T(8,128)(2,1)} %bitcast.38), channel_id=1, source_target_pairs={{0,16},{16,0},{1,17},{17,1},{2,18},{18,2},{3,19},{19,3},{4,20},{20... | collective-permute-start | bytes 12582920 | tf_op jit(solution)/shard_map/ppermute | solution.py:183
  9.5 2.3 %shard_map.86 = bf16[4,2,32,512]{3,2,1,0:T(8,128)(2,1)} custom-call(s32[1,1,2,4,4]{4,3,2,1,0:T(4,128)} %pat.1, bf16[32,1024]{1,0:T(8,128)(2,1)} %bitcast.58, bf16[2,4,512,128]{3,2,1,0:T(8,128)(2,1)} %bitcast.57), custom_call_target="tpu_custom_call" | custom-call | flops 33554432 | bytes 1048576 | tf_op jit(solution)/shard_map/pallas_call | solution.py:156
  11.8 12.0 %all_to_all.5.parts = bf16[4,2,32,512]{3,2,1,0:T(8,128)(2,1)S(1)} all-to-all(bf16[4,2,32,512]{3,2,1,0:T(8,128)(2,1)} %shard_map.86), channel_id=1, replica_groups={{0,1,2,3},{4,5,6,7},{8,9,10,11},{12,13,14,15},{16,17,18,19},{20,21,22,2..., dimensions={0} | all-to-all | bytes 524288 | tf_op jit(solution)/shard_map/all_to_all | solution.py:146
  23.9 7.1 %collective-permute-start.2 = (bf16[1,2,32,512]{3,2,1,0:T(8,128)(2,1)S(1)}, bf16[1,2,32,512]{3,2,1,0:T(8,128)(2,1)S(1)}, u32[]{:S(2)}, u32[]{:S(2)}) collective-permute-start(bf16[1,2,32,512]{3,2,1,0:T(8,128)(2,1)S(1)} %shard_map.87.refs_0_), channel_id=1, source_target_pairs={{0,12},{1,13},{2,14},{3,15},{4,0},{5,1},{6,2},{7,3},{8,4},{9,5},{1... | collective-permute-start | bytes 196616 | tf_op jit(solution)/shard_map/ppermute | solution.py:174
  31.0 2.1 %collective-permute-start.1 = (bf16[1,2,32,512]{3,2,1,0:T(8,128)(2,1)S(1)}, bf16[1,2,32,512]{3,2,1,0:T(8,128)(2,1)S(1)}, u32[]{:S(2)}, u32[]{:S(2)}) collective-permute-start(bf16[1,2,32,512]{3,2,1,0:T(8,128)(2,1)S(1)} %shard_map.87.refs_0_), channel_id=1, source_target_pairs={{0,4},{1,5},{2,6},{3,7},{4,8},{5,9},{6,10},{7,11},{8,12},{9,13},{1... | collective-permute-start | bytes 196616 | tf_op jit(solution)/shard_map/ppermute | solution.py:174
  33.1 10.1 %collective-permute-start = (bf16[1,2,32,512]{3,2,1,0:T(8,128)(2,1)S(1)}, bf16[1,2,32,512]{3,2,1,0:T(8,128)(2,1)S(1)}, u32[]{:S(2)}, u32[]{:S(2)}) collective-permute-start(bf16[1,2,32,512]{3,2,1,0:T(8,128)(2,1)S(1)} %shard_map.87.refs_0_), channel_id=1, source_target_pairs={{0,8},{1,9},{2,10},{3,11},{4,12},{5,13},{6,14},{7,15},{8,0},{9,1},... | collective-permute-start | bytes 196616 | tf_op jit(solution)/shard_map/ppermute | solution.py:174
  43.2 0.1 reshape.38.pat
  43.3 3.5 %collective-permute-done.refs_1_ = bf16[1,2,32,512]{3,2,1,0:T(8,128)(2,1)S(1)} collective-permute-done((bf16[1,2,32,512]{3,2,1,0:T(8,128)(2,1)S(1)}, bf16[1,2,32,512]{3,2,1,0:T(8,128)(2,1)S(1)}, u32[]{:S(2)}, u32[]{:S(2)}) %collective-permute-start) | collective-permute-done | bytes 65568 | tf_op jit(solution)/shard_map/ppermute | solution.py:174
  46.9 4.4 %all-gather = bf16[2,1,32,512]{3,2,1,0:T(8,128)(2,1)S(1)} all-gather(bf16[1,1,32,512]{3,2,1,0:T(8,128)(2,1)S(1)} %fusion), channel_id=2, replica_groups=mesh['col'=16,'row'=2,'leaf'=16] {'row'}, dimensions={0}, use_global_device_ids=true | all-gather | bytes 98304 | tf_op jit(solution)/shard_map/all_gather | solution.py:207
  51.4 1.7 %shard_map.89 = (bf16[1024,1024]{1,0:T(8,128)(2,1)S(1)}, bf16[2,4,512,128]{3,2,1,0:T(8,128)(2,1)S(1)}) custom-call(bf16[4,512,1024]{2,1,0:T(8,128)(2,1)} %bitcast.39, bf16[4,512,1024]{2,1,0:T(8,128)(2,1)} %collective-permute-done.3.other, bf16[4,2,4,512,128]{4,3,2,1,0:T(8,128)(2,1)} %bitcast.48), custom_call_target="tpu_custom_call" | custom-call | bytes 3145728 | tf_op jit(solution)/shard_map/pallas_call | solution.py:194
  53.2 1.7 %shard_map.91 = (f32[32,512]{1,0:T(8,128)S(1)}, bf16[2,32,512]{2,1,0:T(8,128)(2,1)S(1)}, bf16[1024,1024]{1,0:T(8,128)(2,1)S(1)}, bf16[2,4,512,128]{3,2,1,0:T(8,128)(2,1)S(1)}) custom-call(bf16[2,32,512]{2,1,0:T(8,128)(2,1)S(1)} %bitcast.33, f32[2,32,512]{2,1,0:T(8,128)S(1)} %bitcast.30, f32[2,32,512]{2,1,0:T(8,128)S(1)} %bitcast.31, s32[128]{0:T(128)S(1)} %reshape.38.pat, ...), custom_call_target="tpu_custom_call" | custom-call | flops 67108864 | bytes 3145728 | tf_op jit(solution)/shard_map/pallas_call | solution.py:212
  54.9 2.8 %collective-permute-start.5 = (bf16[2,32,512]{2,1,0:T(8,128)(2,1)S(1)}, bf16[2,32,512]{2,1,0:T(8,128)(2,1)S(1)}, u32[]{:S(2)}, u32[]{:S(2)}) collective-permute-start(bf16[2,32,512]{2,1,0:T(8,128)(2,1)S(1)} %get-tuple-element.37), channel_id=1, source_target_pairs={{0,32},{64,96},{128,160},{192,224},{256,288},{320,352},{384,416},{... | collective-permute-start | bytes 196616 | tf_op jit(solution)/shard_map/ppermute | solution.py:241
  57.7 1.3 %collective-permute-start.4 = (bf16[2,32,512]{2,1,0:T(8,128)(2,1)S(1)}, bf16[2,32,512]{2,1,0:T(8,128)(2,1)S(1)}, u32[]{:S(2)}, u32[]{:S(2)}) collective-permute-start(bf16[2,32,512]{2,1,0:T(8,128)(2,1)S(1)} %get-tuple-element.35.refs_1_), channel_id=1, source_target_pairs={{32,64},{96,128},{160,192},{224,256},{288,320},{352,384},{416,448}... | collective-permute-start | bytes 196616 | tf_op jit(solution)/shard_map/ppermute | solution.py:241
  59.0 7.0 %collective-permute-done.4.carry = bf16[2,32,512]{2,1,0:T(8,128)(2,1)S(1)} collective-permute-done((bf16[2,32,512]{2,1,0:T(8,128)(2,1)S(1)}, bf16[2,32,512]{2,1,0:T(8,128)(2,1)S(1)}, u32[]{:S(2)}, u32[]{:S(2)}) %collective-permute-start.4) | collective-permute-done | bytes 65568 | tf_op jit(solution)/shard_map/ppermute | solution.py:241
  66.1 3.3 %all_gather.17.whole = bf16[2,32,512]{2,1,0:T(8,128)(2,1)S(1)} all-gather(bf16[1,32,512]{2,1,0:T(8,128)(2,1)S(1)} %fusion.3), channel_id=1, replica_groups=mesh['col'=16,'row'=2,'leaf'=16] {'row'}, dimensions={0}, use_global_device_ids=true | all-gather | bytes 98304 | tf_op jit(solution)/shard_map/all_gather | solution.py:207
  69.4 1.7 %shard_map.93 = (f32[32,512]{1,0:T(8,128)S(1)}, bf16[2,32,512]{2,1,0:T(8,128)(2,1)S(1)}, bf16[1024,1024]{1,0:T(8,128)(2,1)S(1)}, bf16[2,4,512,128]{3,2,1,0:T(8,128)(2,1)S(1)}) custom-call(bf16[2,32,512]{2,1,0:T(8,128)(2,1)S(1)} %all_gather.17.whole, bf16[2,32,512]{2,1,0:T(8,128)(2,1)S(1)} %collective-permute-done.4.carry, ...), custom_call_target="tpu_custom_call" | custom-call | flops 67108864 | bytes 3145728 | tf_op jit(solution)/shard_map/pallas_call | solution.py:212
  71.2 1.3 %collective-permute-start.7 = (bf16[2,32,512]{2,1,0:T(8,128)(2,1)S(1)}, bf16[2,32,512]{2,1,0:T(8,128)(2,1)S(1)}, u32[]{:S(2)}, u32[]{:S(2)}) collective-permute-start(bf16[2,32,512]{2,1,0:T(8,128)(2,1)S(1)} %get-tuple-element.45), channel_id=1, source_target_pairs={{0,32},{64,96},{128,160},{192,224},{256,288},{320,352},{384,416},{... | collective-permute-start | bytes 196616 | tf_op jit(solution)/shard_map/ppermute | solution.py:241
  72.5 1.3 %collective-permute-start.6 = (bf16[2,32,512]{2,1,0:T(8,128)(2,1)S(1)}, bf16[2,32,512]{2,1,0:T(8,128)(2,1)S(1)}, u32[]{:S(2)}, u32[]{:S(2)}) collective-permute-start(bf16[2,32,512]{2,1,0:T(8,128)(2,1)S(1)} %get-tuple-element.41.refs_1_), channel_id=1, source_target_pairs={{32,64},{96,128},{160,192},{224,256},{288,320},{352,384},{416,448}... | collective-permute-start | bytes 196616 | tf_op jit(solution)/shard_map/ppermute | solution.py:241
  73.8 7.0 %collective-permute-done.6.carry = bf16[2,32,512]{2,1,0:T(8,128)(2,1)S(1)} collective-permute-done((bf16[2,32,512]{2,1,0:T(8,128)(2,1)S(1)}, bf16[2,32,512]{2,1,0:T(8,128)(2,1)S(1)}, u32[]{:S(2)}, u32[]{:S(2)}) %collective-permute-start.6) | collective-permute-done | bytes 65568 | tf_op jit(solution)/shard_map/ppermute | solution.py:241
  80.8 3.0 %all_gather.18.whole = bf16[2,32,512]{2,1,0:T(8,128)(2,1)S(1)} all-gather(bf16[1,32,512]{2,1,0:T(8,128)(2,1)S(1)} %fusion.2), channel_id=1, replica_groups=mesh['col'=16,'row'=2,'leaf'=16] {'row'}, dimensions={0}, use_global_device_ids=true | all-gather | bytes 98304 | tf_op jit(solution)/shard_map/all_gather | solution.py:207
  83.9 1.7 %shard_map.95 = (f32[32,512]{1,0:T(8,128)S(1)}, bf16[2,32,512]{2,1,0:T(8,128)(2,1)S(1)}, bf16[1024,1024]{1,0:T(8,128)(2,1)S(1)}, bf16[2,4,512,128]{3,2,1,0:T(8,128)(2,1)S(1)}) custom-call(bf16[2,32,512]{2,1,0:T(8,128)(2,1)S(1)} %all_gather.18.whole, bf16[2,32,512]{2,1,0:T(8,128)(2,1)S(1)} %collective-permute-done.6.carry, ...), custom_call_target="tpu_custom_call" | custom-call | flops 67108864 | bytes 3145728 | tf_op jit(solution)/shard_map/pallas_call | solution.py:212
  85.6 1.3 %collective-permute-start.9 = (bf16[2,32,512]{2,1,0:T(8,128)(2,1)S(1)}, bf16[2,32,512]{2,1,0:T(8,128)(2,1)S(1)}, u32[]{:S(2)}, u32[]{:S(2)}) collective-permute-start(bf16[2,32,512]{2,1,0:T(8,128)(2,1)S(1)} %get-tuple-element.53), channel_id=1, source_target_pairs={{0,32},{64,96},{128,160},{192,224},{256,288},{320,352},{384,416},{... | collective-permute-start | bytes 196616 | tf_op jit(solution)/shard_map/ppermute | solution.py:241
  86.9 1.3 %collective-permute-start.8 = (bf16[2,32,512]{2,1,0:T(8,128)(2,1)S(1)}, bf16[2,32,512]{2,1,0:T(8,128)(2,1)S(1)}, u32[]{:S(2)}, u32[]{:S(2)}) collective-permute-start(bf16[2,32,512]{2,1,0:T(8,128)(2,1)S(1)} %get-tuple-element.49.refs_1_), channel_id=1, source_target_pairs={{32,64},{96,128},{160,192},{224,256},{288,320},{352,384},{416,448}... | collective-permute-start | bytes 196616 | tf_op jit(solution)/shard_map/ppermute | solution.py:241
  88.2 7.0 %collective-permute-done.8.carry = bf16[2,32,512]{2,1,0:T(8,128)(2,1)S(1)} collective-permute-done((bf16[2,32,512]{2,1,0:T(8,128)(2,1)S(1)}, bf16[2,32,512]{2,1,0:T(8,128)(2,1)S(1)}, u32[]{:S(2)}, u32[]{:S(2)}) %collective-permute-start.8) | collective-permute-done | bytes 65568 | tf_op jit(solution)/shard_map/ppermute | solution.py:241
  95.3 3.0 %all_gather.19.whole = bf16[2,32,512]{2,1,0:T(8,128)(2,1)S(1)} all-gather(bf16[1,32,512]{2,1,0:T(8,128)(2,1)S(1)} %fusion.1), channel_id=1, replica_groups=mesh['col'=16,'row'=2,'leaf'=16] {'row'}, dimensions={0}, use_global_device_ids=true | all-gather | bytes 98304 | tf_op jit(solution)/shard_map/all_gather | solution.py:207
  98.3 1.3 %collective-permute-start.10 = (bf16[2,32,512]{2,1,0:T(8,128)(2,1)S(1)}, bf16[2,32,512]{2,1,0:T(8,128)(2,1)S(1)}, u32[]{:S(2)}, u32[]{:S(2)}) collective-permute-start(bf16[2,32,512]{2,1,0:T(8,128)(2,1)S(1)} %get-tuple-element.57.refs_1_), channel_id=1, source_target_pairs={{32,64},{96,128},{160,192},{224,256},{288,320},{352,384},{416,448}... | collective-permute-start | bytes 196616 | tf_op jit(solution)/shard_map/ppermute | solution.py:241
  99.6 1.6 %shard_map.97 = (f32[32,512]{1,0:T(8,128)S(1)}, bf16[2,32,512]{2,1,0:T(8,128)(2,1)S(1)}) custom-call(bf16[2,32,512]{2,1,0:T(8,128)(2,1)S(1)} %all_gather.19.whole, bf16[2,32,512]{2,1,0:T(8,128)(2,1)S(1)} %collective-permute-done.8.carry, bf16[2,32,512]{2,1,0:T(8,128)(2,1)S(1)} %collective-permute-done.9.late, s32[128]{0:T(128)S(1)} %reshape.38.pat, ...), custom_call_target="tpu_custom_call" | custom-call | flops 67108864 | bytes 3145728 | tf_op jit(solution)/shard_map/pallas_call | solution.py:212
  101.2 1.3 %collective-permute-start.11 = (bf16[2,32,512]{2,1,0:T(8,128)(2,1)S(1)}, bf16[2,32,512]{2,1,0:T(8,128)(2,1)S(1)}, u32[]{:S(2)}, u32[]{:S(2)}) collective-permute-start(bf16[2,32,512]{2,1,0:T(8,128)(2,1)S(1)} %get-tuple-element.61), channel_id=1, source_target_pairs={{0,32},{64,96},{128,160},{192,224},{256,288},{320,352},{384,416},{... | collective-permute-start | bytes 196616 | tf_op jit(solution)/shard_map/ppermute | solution.py:241
  102.5 0.7 maximum_bitcast_fusion
  103.3 0.6 collective-permute-done.11
  103.8 2.8 %collective-permute-done.10 = bf16[2,32,512]{2,1,0:T(8,128)(2,1)S(1)} collective-permute-done((bf16[2,32,512]{2,1,0:T(8,128)(2,1)S(1)}, bf16[2,32,512]{2,1,0:T(8,128)(2,1)S(1)}, u32[]{:S(2)}, u32[]{:S(2)}) %collective-permute-start.10) | collective-permute-done | bytes 65568 | tf_op jit(solution)/shard_map/ppermute | solution.py:241
  106.7 0.7 add_bitcast_fusion
  (20 shorter events, 0.4 us)
Async XLA Ops:
  0.6 42.6 %copy-start.1 = (s32[4,1,2,4,4]{4,3,2,1,0:T(4,128)S(1)}, s32[4,1,2,4,4]{4,3,2,1,0:T(4,128)}, u32[]{:S(2)}) copy-start(s32[4,1,2,4,4]{4,3,2,1,0:T(4,128)} %param.10) | copy-start | bytes 1540
  0.6 46.3 %copy-start = (f32[4,1,32,512]{3,2,1,0:T(8,128)S(1)}, f32[4,1,32,512]{3,2,1,0:T(8,128)}, u32[]{:S(2)}) copy-start(f32[4,1,32,512]{3,2,1,0:T(8,128)} %param.7) | copy-start | bytes 786436
  0.7 50.7 %collective-permute-start.3 = (bf16[4,512,1024]{2,1,0:T(8,128)(2,1)}, bf16[4,512,1024]{2,1,0:T(8,128)(2,1)}, u32[]{:S(2)}, u32[]{:S(2)}) collective-permute-start(bf16[4,512,1024]{2,1,0:T(8,128)(2,1)} %bitcast.38), channel_id=1, source_target_pairs={{0,16},{16,0},{1,17},{17,1},{2,18},{18,2},{3,19},{19,3},{4,20},{20... | collective-permute-start | bytes 12582920 | tf_op jit(solution)/shard_map/ppermute | solution.py:183
  23.9 19.4 %collective-permute-start.2 = (bf16[1,2,32,512]{3,2,1,0:T(8,128)(2,1)S(1)}, bf16[1,2,32,512]{3,2,1,0:T(8,128)(2,1)S(1)}, u32[]{:S(2)}, u32[]{:S(2)}) collective-permute-start(bf16[1,2,32,512]{3,2,1,0:T(8,128)(2,1)S(1)} %shard_map.87.refs_0_), channel_id=1, source_target_pairs={{0,12},{1,13},{2,14},{3,15},{4,0},{5,1},{6,2},{7,3},{8,4},{9,5},{1... | collective-permute-start | bytes 196616 | tf_op jit(solution)/shard_map/ppermute | solution.py:174
  31.0 12.3 %collective-permute-start.1 = (bf16[1,2,32,512]{3,2,1,0:T(8,128)(2,1)S(1)}, bf16[1,2,32,512]{3,2,1,0:T(8,128)(2,1)S(1)}, u32[]{:S(2)}, u32[]{:S(2)}) collective-permute-start(bf16[1,2,32,512]{3,2,1,0:T(8,128)(2,1)S(1)} %shard_map.87.refs_0_), channel_id=1, source_target_pairs={{0,4},{1,5},{2,6},{3,7},{4,8},{5,9},{6,10},{7,11},{8,12},{9,13},{1... | collective-permute-start | bytes 196616 | tf_op jit(solution)/shard_map/ppermute | solution.py:174
  33.1 13.8 %collective-permute-start = (bf16[1,2,32,512]{3,2,1,0:T(8,128)(2,1)S(1)}, bf16[1,2,32,512]{3,2,1,0:T(8,128)(2,1)S(1)}, u32[]{:S(2)}, u32[]{:S(2)}) collective-permute-start(bf16[1,2,32,512]{3,2,1,0:T(8,128)(2,1)S(1)} %shard_map.87.refs_0_), channel_id=1, source_target_pairs={{0,8},{1,9},{2,10},{3,11},{4,12},{5,13},{6,14},{7,15},{8,0},{9,1},... | collective-permute-start | bytes 196616 | tf_op jit(solution)/shard_map/ppermute | solution.py:174
  54.9 4.1 %collective-permute-start.5 = (bf16[2,32,512]{2,1,0:T(8,128)(2,1)S(1)}, bf16[2,32,512]{2,1,0:T(8,128)(2,1)S(1)}, u32[]{:S(2)}, u32[]{:S(2)}) collective-permute-start(bf16[2,32,512]{2,1,0:T(8,128)(2,1)S(1)} %get-tuple-element.37), channel_id=1, source_target_pairs={{0,32},{64,96},{128,160},{192,224},{256,288},{320,352},{384,416},{... | collective-permute-start | bytes 196616 | tf_op jit(solution)/shard_map/ppermute | solution.py:241
  57.7 8.3 %collective-permute-start.4 = (bf16[2,32,512]{2,1,0:T(8,128)(2,1)S(1)}, bf16[2,32,512]{2,1,0:T(8,128)(2,1)S(1)}, u32[]{:S(2)}, u32[]{:S(2)}) collective-permute-start(bf16[2,32,512]{2,1,0:T(8,128)(2,1)S(1)} %get-tuple-element.35.refs_1_), channel_id=1, source_target_pairs={{32,64},{96,128},{160,192},{224,256},{288,320},{352,384},{416,448}... | collective-permute-start | bytes 196616 | tf_op jit(solution)/shard_map/ppermute | solution.py:241
  71.2 2.6 %collective-permute-start.7 = (bf16[2,32,512]{2,1,0:T(8,128)(2,1)S(1)}, bf16[2,32,512]{2,1,0:T(8,128)(2,1)S(1)}, u32[]{:S(2)}, u32[]{:S(2)}) collective-permute-start(bf16[2,32,512]{2,1,0:T(8,128)(2,1)S(1)} %get-tuple-element.45), channel_id=1, source_target_pairs={{0,32},{64,96},{128,160},{192,224},{256,288},{320,352},{384,416},{... | collective-permute-start | bytes 196616 | tf_op jit(solution)/shard_map/ppermute | solution.py:241
  72.5 8.3 %collective-permute-start.6 = (bf16[2,32,512]{2,1,0:T(8,128)(2,1)S(1)}, bf16[2,32,512]{2,1,0:T(8,128)(2,1)S(1)}, u32[]{:S(2)}, u32[]{:S(2)}) collective-permute-start(bf16[2,32,512]{2,1,0:T(8,128)(2,1)S(1)} %get-tuple-element.41.refs_1_), channel_id=1, source_target_pairs={{32,64},{96,128},{160,192},{224,256},{288,320},{352,384},{416,448}... | collective-permute-start | bytes 196616 | tf_op jit(solution)/shard_map/ppermute | solution.py:241
  85.6 2.6 %collective-permute-start.9 = (bf16[2,32,512]{2,1,0:T(8,128)(2,1)S(1)}, bf16[2,32,512]{2,1,0:T(8,128)(2,1)S(1)}, u32[]{:S(2)}, u32[]{:S(2)}) collective-permute-start(bf16[2,32,512]{2,1,0:T(8,128)(2,1)S(1)} %get-tuple-element.53), channel_id=1, source_target_pairs={{0,32},{64,96},{128,160},{192,224},{256,288},{320,352},{384,416},{... | collective-permute-start | bytes 196616 | tf_op jit(solution)/shard_map/ppermute | solution.py:241
  86.9 8.3 %collective-permute-start.8 = (bf16[2,32,512]{2,1,0:T(8,128)(2,1)S(1)}, bf16[2,32,512]{2,1,0:T(8,128)(2,1)S(1)}, u32[]{:S(2)}, u32[]{:S(2)}) collective-permute-start(bf16[2,32,512]{2,1,0:T(8,128)(2,1)S(1)} %get-tuple-element.49.refs_1_), channel_id=1, source_target_pairs={{32,64},{96,128},{160,192},{224,256},{288,320},{352,384},{416,448}... | collective-permute-start | bytes 196616 | tf_op jit(solution)/shard_map/ppermute | solution.py:241
  98.3 8.3 %collective-permute-start.10 = (bf16[2,32,512]{2,1,0:T(8,128)(2,1)S(1)}, bf16[2,32,512]{2,1,0:T(8,128)(2,1)S(1)}, u32[]{:S(2)}, u32[]{:S(2)}) collective-permute-start(bf16[2,32,512]{2,1,0:T(8,128)(2,1)S(1)} %get-tuple-element.57.refs_1_), channel_id=1, source_target_pairs={{32,64},{96,128},{160,192},{224,256},{288,320},{352,384},{416,448}... | collective-permute-start | bytes 196616 | tf_op jit(solution)/shard_map/ppermute | solution.py:241
  101.2 2.6 %collective-permute-start.11 = (bf16[2,32,512]{2,1,0:T(8,128)(2,1)S(1)}, bf16[2,32,512]{2,1,0:T(8,128)(2,1)S(1)}, u32[]{:S(2)}, u32[]{:S(2)}) collective-permute-start(bf16[2,32,512]{2,1,0:T(8,128)(2,1)S(1)} %get-tuple-element.61), channel_id=1, source_target_pairs={{0,32},{64,96},{128,160},{192,224},{256,288},{320,352},{384,416},{... | collective-permute-start | bytes 196616 | tf_op jit(solution)/shard_map/ppermute | solution.py:241
